TPU v7x, 32 devices: a whole 2x2x4 slice. The times are simulated.
32 devices in a mesh: section: 4 (over z), row: 2 (over y), col: 4 (over x, core).
Axes of the slice: x: 2, y: 2, z: 4, core: 2. Of those that a mesh axis runs over, the one named last changes fastest.
Arguments:
- tokens: bfloat16 [4, 128, 3072], P('section', 'col', 'row'), may hold values from -6 to 6
- weights: bfloat16 [4, 3072, 12288], P('section', 'row', 'col'), may hold values from -0.109375 to 0.109375
- hidden_grads: bfloat16 [4, 128, 12288], P('section', 'row', 'col'), may hold values from -1.5 to 1.5
Outputs:
- hidden: bfloat16 [4, 128, 12288], P('section', 'row', 'col')
- weight_grad: bfloat16 [4, 3072, 12288], P('section', 'row', 'col')
- passed_grad: bfloat16 [4, 128, 3072], P('section', 'col', 'row')
All inputs are finite; a program needn't handle non-finite values.
Results may differ from a plain program's by a relative error of at most 0.0052.
Values may be sent and summed in bfloat16 or wider, within the bound.
No kernel may reach another device: no remote copies, remote signals or barrier semaphores. Data moves between devices by JAX's collectives and lax.ppermute only.
A program may use at most 64 MiB of HBM per device.

v0:
```python
import jax
import jax.numpy as jnp
from jax import lax
from jax.sharding import PartitionSpec as P


def shifted(value, axis, steps):
    count = lax.axis_size(axis)
    leading, last = (max(0, -steps), min(count, count - steps))
    return lax.ppermute(value, axis, [(source, source + steps) for source in range(leading, last)])


def on_device(tokens, weights, hidden_grads):
    token_tile = tokens[0]
    weight_tile = weights[0]
    grad_tile = hidden_grads[0]
    tokens_all = lax.all_gather(token_tile, "col", axis=0, tiled=True)
    hidden_sum = lax.psum_scatter(
        jnp.dot(tokens_all, weight_tile, preferred_element_type=jnp.float32).astype(jnp.bfloat16),
        "row",
        scatter_dimension=0,
        tiled=True,
    )
    grad_piece = lax.all_gather(grad_tile, "row", axis=0, tiled=True)
    weight_total = lax.dot_general(
        tokens_all, grad_piece, (((0,), (0,)), ((), ())), preferred_element_type=jnp.float32
    )
    input_piece = lax.dot_general(
        grad_piece, weight_tile, (((1,), (1,)), ((), ())), preferred_element_type=jnp.float32
    )
    weight_grad = weight_total.astype(jnp.bfloat16)
    input_grad = lax.psum_scatter(input_piece, "col", scatter_dimension=0, tiled=True).astype(
        jnp.bfloat16
    )
    passed_grad = shifted(input_grad, "section", -1)
    return (hidden_sum[None], weight_grad[None], passed_grad[None])


def solution(mesh):
    in_specs = (P("section", "col", "row"), P("section", "row", "col"), P("section", "row", "col"))
    out_specs = (P("section", "row", "col"), P("section", "row", "col"), P("section", "col", "row"))
    return jax.shard_map(
        on_device, mesh=mesh, in_specs=in_specs, out_specs=out_specs, check_vma=False
    )
```

profile of v0, /device:TPU:0, one launch (start us, length us, event | category | flops | bytes accessed | tf_op | source)
XLA Modules:
  0.0 80.7 jit_solution(3190279994158967588)
XLA Ops:
  7.2 0.0 copy-start
  7.2 0.0 reduce-scatter.5.cloned.1.call-start
  7.2 13.0 %all-gather.1 = bf16[1,128,3072]{2,1,0:T(8,128)(2,1)S(1)} all-gather(bf16[1,64,3072]{2,1,0:T(8,128)(2,1)} %param.5), channel_id=3, replica_groups=mesh['section'=4,'row'=2,'col'=4] {'row'}, dimensions={1}, use_global_device_ids=true | all-gather | bytes 1179648 | tf_op jit(solution)/shard_map/all_gather | solution.py:24
  20.2 7.8 %fusion.1 = f32[128,1536]{1,0:T(8,128)} fusion(bf16[1,1536,3072]{2,1,0:T(8,128)(2,1)} %param.4, bf16[1,128,3072]{2,1,0:T(8,128)(2,1)S(1)} %all-gather.1), kind=kOutput, calls=%fused_computation.2 | convolution fusion | flops 1207959552 | bytes 11010048 | tf_op jit(solution)/shard_map/dot_general | solution.py:28
  28.0 0.0 reduce-scatter.5.cloned.1.call-update
  28.0 0.0 reduce-scatter.3.cloned.1.call-start
  28.1 0.0 copy-done
  28.1 6.6 %all-gather = bf16[1,128,1536]{2,1,0:T(8,128)(2,1)S(1)} all-gather(bf16[1,32,1536]{2,1,0:T(8,128)(2,1)S(1)} %copy-done), channel_id=2, replica_groups=mesh['section'=4,'row'=2,'col'=4] {'col'}, dimensions={1}, use_global_device_ids=true | all-gather | bytes 491520 | tf_op jit(solution)/shard_map/all_gather | solution.py:17
  34.7 6.2 %fusion.5 = bf16[128,3072]{1,0:T(8,128)(2,1)} fusion(bf16[1,1536,3072]{2,1,0:T(8,128)(2,1)} %param.4, bf16[1,128,1536]{2,1,0:T(8,128)(2,1)S(1)} %all-gather), kind=kOutput, calls=%fused_computation.6 | convolution fusion | flops 1208352768 | bytes 10616832 | tf_op jit(solution)/shard_map/dot_general | solution.py:19
  41.0 0.0 reduce-scatter.3.cloned.1.call-update
  41.0 11.9 %reduce-scatter.5.cloned.1.call-done = f32[32,1536]{1,0:T(8,128)} async-done(((f32[128,1536]{1,0:T(8,128)}), f32[32,1536]{1,0:T(8,128)}) %reduce-scatter.5.cloned.1.call-update) | async-done | bytes 196624 | tf_op jit(solution)/shard_map/reduce_scatter | solution.py:32
  52.9 0.9 %convert_element_type.11 = bf16[32,1536]{1,0:T(8,128)(2,1)S(1)} convert(f32[32,1536]{1,0:T(8,128)} %reduce-scatter.5.cloned.1.call-done) | non-fusion elementwise | flops 49152 | bytes 294912 | tf_op jit(solution)/shard_map/convert_element_type | solution.py:32
  53.8 1.3 %collective-permute-start = (bf16[32,1536]{1,0:T(8,128)(2,1)S(1)}, bf16[32,1536]{1,0:T(8,128)(2,1)S(1)}, u32[]{:S(2)}, u32[]{:S(2)}) collective-permute-start(bf16[32,1536]{1,0:T(8,128)(2,1)S(1)} %convert_element_type.11), channel_id=1, source_target_pairs={{8,0},{16,8},{24,16},{9,1},{17,9},{25,17},{10,2},{18,10},{26,18},{... | collective-permute-start | bytes 294920 | tf_op jit(solution)/shard_map/ppermute | solution.py:10
  55.1 5.2 %fusion = bf16[1,1536,3072]{2,1,0:T(8,128)(2,1)} fusion(bf16[1,128,3072]{2,1,0:T(8,128)(2,1)S(1)} %all-gather.1, bf16[1,128,1536]{2,1,0:T(8,128)(2,1)S(1)} %all-gather), kind=kOutput, calls=%fused_computation.1 | convolution fusion | flops 1212678144 | bytes 10616832 | tf_op jit(solution)/shard_map/dot_general | solution.py:25
  60.3 0.0 collective-permute-done
  60.3 12.9 %reduce-scatter.3.cloned.1.call-done = bf16[64,3072]{1,0:T(8,128)(2,1)} async-done(((bf16[128,3072]{1,0:T(8,128)(2,1)}), bf16[64,3072]{1,0:T(8,128)(2,1)}) %reduce-scatter.3.cloned.1.call-update) | async-done | bytes 393232 | tf_op jit(solution)/shard_map/reduce_scatter | solution.py:18
  73.3 0.6 copy.7
Async XLA Ops:
  7.2 20.9 %copy-start = (bf16[1,32,1536]{2,1,0:T(8,128)(2,1)S(1)}, bf16[1,32,1536]{2,1,0:T(8,128)(2,1)}, u32[]{:S(2)}) copy-start(bf16[1,32,1536]{2,1,0:T(8,128)(2,1)} %param.3) | copy-start | bytes 294916
  7.2 45.7 %reduce-scatter.5.cloned.1.call-start = ((), (), s32[]{:S(2)}) async-start(), calls=%async_computation.3 | async-start | bytes 983040 | tf_op jit(solution)/shard_map/reduce_scatter | solution.py:32
  28.0 45.2 %reduce-scatter.3.cloned.1.call-start = ((), (), s32[]{:S(2)}) async-start(), calls=%async_computation.2 | async-start | bytes 1179648 | tf_op jit(solution)/shard_map/reduce_scatter | solution.py:18
  53.8 6.5 %collective-permute-start = (bf16[32,1536]{1,0:T(8,128)(2,1)S(1)}, bf16[32,1536]{1,0:T(8,128)(2,1)S(1)}, u32[]{:S(2)}, u32[]{:S(2)}) collective-permute-start(bf16[32,1536]{1,0:T(8,128)(2,1)S(1)} %convert_element_type.11), channel_id=1, source_target_pairs={{8,0},{16,8},{24,16},{9,1},{17,9},{25,17},{10,2},{18,10},{26,18},{... | collective-permute-start | bytes 294920 | tf_op jit(solution)/shard_map/ppermute | solution.py:10
Sparse Core Ops, SparseCore 0:
  28.2 24.6 reduce-scatter.4
  55.8 17.4 reduce-scatter.2
where the time goes:
time: 81 us; the launch traced here: 80.7 us
  waiting for transfers between devices  24.9 us (31%)
  blocking collectives  19.7 us (24%)
  matrix products  19.2 us (24%)
  between operations  14.1 us (17%)
  starting transfers between devices  1.37 us (2%)
  other arithmetic  0.94 us (1%)
    all_gather x1, blocking collectives, on_device(): grad_piece = lax.all_gather(grad_tile, 'row', axis=0, tiled=True)  13 us
    reduce_scatter x1, waiting for transfers between devices, on_device(): lax.psum_scatter(jnp.dot(tokens_all, weight_tile, preferred_element_type=...  12.9 us
    reduce_scatter x1, waiting for transfers between devices, on_device(): lax.psum_scatter(input_piece, 'col', scatter_dimension=0, tiled=True)  11.9 us
    dot_general x1, matrix products, on_device(): lax.dot_general(grad_piece, weight_tile, (((1,), (1,)), ((), ())), prefer...  7.78 us
    all_gather x1, blocking collectives, on_device(): tokens_all = lax.all_gather(token_tile, 'col', axis=0, tiled=True)  6.64 us
    dot_general x1, matrix products, on_device(): jnp.dot(tokens_all, weight_tile, preferred_element_type=jnp.float32)  6.23 us
    dot_general x1, matrix products, on_device(): lax.dot_general(tokens_all, grad_piece, (((0,), (0,)), ((), ())), preferr...  5.17 us
  transfers between devices with their start and end apart: 3, of which 2 were waited for; matrix products, arithmetic and copies ran while one was open for 15% of the time, Pallas kernels for 0%

commit v1 on v0

v1 whole, which is shorter than its diff:
```python
import functools

import jax
import jax.numpy as jnp
from jax import lax
from jax.experimental import pallas as pl
from jax.experimental.pallas import tpu as pltpu
from jax.sharding import PartitionSpec as P

F32 = jnp.float32
BF16 = jnp.bfloat16
VMEM = pl.BlockSpec(memory_space=pltpu.VMEM)
MIB = 1 << 20


def shifted(value, axis, steps):
    count = lax.axis_size(axis)
    leading, last = (max(0, -steps), min(count, count - steps))
    return lax.ppermute(value, axis, [(source, source + steps) for source in range(leading, last)])


def swapped(value, axis, distance):
    count = lax.axis_size(axis)
    return lax.ppermute(value, axis, [(source, source ^ distance) for source in range(count)])


def general_step(tokens, weights, hidden_grads):
    token_tile, weight_tile, grad_tile = tokens[0], weights[0], hidden_grads[0]
    tokens_all = lax.all_gather(token_tile, "col", axis=0, tiled=True)
    hidden_sum = lax.psum_scatter(
        jnp.dot(tokens_all, weight_tile, preferred_element_type=F32).astype(BF16),
        "row",
        scatter_dimension=0,
        tiled=True,
    )
    grad_piece = lax.all_gather(grad_tile, "row", axis=0, tiled=True)
    weight_grad = lax.dot_general(
        tokens_all, grad_piece, (((0,), (0,)), ((), ())), preferred_element_type=F32
    ).astype(BF16)
    input_piece = lax.dot_general(
        grad_piece, weight_tile, (((1,), (1,)), ((), ())), preferred_element_type=F32
    )
    input_grad = lax.psum_scatter(input_piece, "col", scatter_dimension=0, tiled=True).astype(BF16)
    return (hidden_sum[None], weight_grad[None], shifted(input_grad, "section", -1)[None])


def call(kernel, out_shapes, args, scratch=(), flops=0, moved=0, name=None, grid=(), in_specs=None, out_specs=None):
    single = not isinstance(out_shapes, (list, tuple))
    shapes = [out_shapes] if single else list(out_shapes)
    in_specs = in_specs or [VMEM] * len(args)
    out_specs = out_specs or [VMEM] * len(shapes)
    result = pl.pallas_call(
        kernel,
        grid=grid,
        out_shape=shapes,
        in_specs=in_specs,
        out_specs=out_specs,
        scratch_shapes=list(scratch),
        compiler_params=pltpu.CompilerParams(vmem_limit_bytes=16 * MIB),
        cost_estimate=pl.CostEstimate(flops=flops, bytes_accessed=moved, transcendentals=0),
        name=name,
    )(*args)
    return result[0] if single else result


def forward_kernel(own, beside, across, diagonal, weight, tokens_out, send_out, keep_out, *, tile):
    rows = own.shape[0]
    row, col = lax.axis_index("row"), lax.axis_index("col")
    chip, core = col // 2, col % 2
    near = jnp.where(chip == row, 2 * rows, 0)
    far = 2 * rows - near
    for ref, start in (
        (own, near + core * rows),
        (beside, near + (1 - core) * rows),
        (across, far + core * rows),
        (diagonal, far + (1 - core) * rows),
    ):
        tokens_out[pl.ds(pl.multiple_of(start, rows), rows), :] = ref[...]
    half = 2 * rows
    for lower in range(0, weight.shape[1], tile):
        product = jnp.dot(
            tokens_out[...], weight[:, lower : lower + tile], preferred_element_type=F32
        ).astype(BF16)
        send_out[:, lower : lower + tile] = product[:half]
        keep_out[:, lower : lower + tile] = product[half:]


def input_grad_kernel(other, own, weight, send_out, keep_out, total, *, tile):
    rows = own.shape[0] // 2
    core = lax.axis_index("col") % 2
    grads = jnp.concatenate([other[...], own[...]], axis=0)
    for lower in range(0, weight.shape[0], tile):
        total[:, lower : lower + tile] = lax.dot_general(
            grads,
            weight[lower : lower + tile, :],
            (((1,), (1,)), ((), ())),
            preferred_element_type=F32,
        )
    for half in range(2):
        mine = pl.multiple_of(2 * half * rows + core * rows, rows)
        theirs = pl.multiple_of(2 * half * rows + (1 - core) * rows, rows)
        keep_out[half * rows : (half + 1) * rows, :] = total[pl.ds(mine, rows), :]
        send_out[half * rows : (half + 1) * rows, :] = total[pl.ds(theirs, rows), :].astype(BF16)


def pair_kernel(keep, received, straight_out, across_out):
    rows = keep.shape[0] // 2
    straight = pl.multiple_of(
        jnp.where(lax.axis_index("col") // 2 == lax.axis_index("row"), rows, 0), rows
    )
    across = pl.multiple_of(rows - straight, rows)
    straight_out[...] = (
        keep[pl.ds(straight, rows), :] + received[pl.ds(straight, rows), :].astype(F32)
    ).astype(BF16)
    across_out[...] = (
        keep[pl.ds(across, rows), :] + received[pl.ds(across, rows), :].astype(F32)
    ).astype(BF16)


def weight_grad_kernel(tokens, other, own, out):
    grads = jnp.concatenate([other[...], own[...]], axis=0)
    out[...] = lax.dot_general(
        tokens[...], grads, (((0,), (0,)), ((), ())), preferred_element_type=F32
    ).astype(BF16)


def paired_step(tokens, weights, hidden_grads):
    own, weight, grads = tokens[0], weights[0], hidden_grads[0]
    rows, width = own.shape
    half, units = grads.shape
    sections = lax.axis_size("section")
    columns = lax.axis_size("col")
    grads_other = swapped(grads, "row", 1)
    across = swapped(own, "col", 2)
    beside = swapped(own, "col", 1)
    diagonal = swapped(across, "col", 1)
    flops = 4 * half * width * units
    tokens_all, hidden_send, hidden_keep = call(
        functools.partial(forward_kernel, tile=512),
        [
            jax.ShapeDtypeStruct((4 * rows, width), BF16),
            jax.ShapeDtypeStruct((half, units), BF16),
            jax.ShapeDtypeStruct((half, units), BF16),
        ],
        (own, beside, across, diagonal, weight),
        flops=flops,
        moved=2 * width * units,
        name="forward",
    )
    hidden_received = swapped(hidden_send, "row", 1)
    piece_send, piece_keep = call(
        functools.partial(input_grad_kernel, tile=256),
        [
            jax.ShapeDtypeStruct((half, width), BF16),
            jax.ShapeDtypeStruct((half, width), F32),
        ],
        (grads_other, grads, weight),
        scratch=[pltpu.VMEM((2 * half, width), F32)],
        flops=flops,
        moved=2 * width * units,
        name="input_grad",
    )
    piece_received = swapped(piece_send, "col", 1)
    straight, crossing = call(
        pair_kernel,
        [jax.ShapeDtypeStruct((rows, width), BF16)] * 2,
        (piece_keep, piece_received),
        moved=8 * half * width,
        name="pair_sum",
    )
    tokens_late, straight, crossing = lax.optimization_barrier((tokens_all, straight, crossing))
    straight_received = shifted(straight, "section", -1)
    crossing_received = lax.ppermute(
        crossing,
        ("section", "col"),
        [
            (section * columns + col, (section - 1) * columns + (col ^ 2))
            for section in range(1, sections)
            for col in range(columns)
        ],
    )
    block = 512
    weight_grad = call(
        weight_grad_kernel,
        jax.ShapeDtypeStruct((width, units), BF16),
        (tokens_late, grads_other, grads),
        grid=(width // block,),
        in_specs=[
            pl.BlockSpec((2 * half, block), lambda step: (0, step)),
            pl.BlockSpec((half, units), lambda step: (0, 0)),
            pl.BlockSpec((half, units), lambda step: (0, 0)),
        ],
        out_specs=[pl.BlockSpec((block, units), lambda step: (step, 0))],
        flops=flops,
        moved=2 * width * units,
        name="weight_grad",
    )
    passed_grad = (straight_received.astype(F32) + crossing_received.astype(F32)).astype(BF16)
    hidden = (hidden_keep.astype(F32) + hidden_received.astype(F32)).astype(BF16)
    return (hidden[None], weight_grad[None], passed_grad[None])


def solution(mesh):
    in_specs = (P("section", "col", "row"), P("section", "row", "col"), P("section", "row", "col"))
    out_specs = (P("section", "row", "col"), P("section", "row", "col"), P("section", "col", "row"))
    paired = mesh.shape["row"] == 2 and mesh.shape["col"] == 4
    return jax.shard_map(
        paired_step if paired else general_step,
        mesh=mesh,
        in_specs=in_specs,
        out_specs=out_specs,
        check_vma=False,
    )
```

time: 81 us -> 34.2 us (0.42)
  blocking collectives: 19.7 us -> 0 us
  matrix products: 19.2 us -> 0 us
  waiting for transfers between devices: 24.9 us -> 7.47 us
  between operations: 14.1 us -> 0.68 us
  Pallas kernels: 0 us -> 10.1 us
  starting transfers between devices: 1.37 us -> 7.47 us
  local copies, waits for them, and re-layouts: 0.64 us -> 6.7 us
    reduce_scatter x2 -> x0, waiting for transfers between devices: 24.8 us -> none  [the longest x1 12.9 us: on_device(): lax.psum_scatter(jnp.dot(tokens_all, weight_tile, preferred_element_type=...]
    all_gather x2 -> x0, blocking collectives: 19.7 us -> none  [the longest x1 13 us: on_device(): grad_piece = lax.all_gather(grad_tile, 'row', axis=0, tiled=True)]
    dot_general x3 -> x0, matrix products: 19.2 us -> none  [the longest x1 7.78 us: on_device(): lax.dot_general(grad_piece, weight_tile, (((1,), (1,)), ((), ())), prefer...]
    pallas_call x0 -> x4, Pallas kernels: none -> 10.1 us  [call(): pl.pallas_call(kernel, grid=grid, out_shape=shapes, in_specs=in_specs, ou...]
    ppermute x0 -> x7, waiting for transfers between devices: none -> 7.46 us  [the longest x6 7.46 us: swapped(): lax.ppermute(value, axis, [(source, source ^ distance) for source in rang...]
    ppermute x0 -> x7, starting transfers between devices: none -> 6.18 us  [the longest x6 4.88 us: swapped(): lax.ppermute(value, axis, [(source, source ^ distance) for source in rang...]
    unnamed x3 -> x8, local copies, waits for them, and re-layouts: 0.64 us -> 6.7 us
    broadcast_in_dim x0 -> x2, other arithmetic: none -> 1.51 us  [paired_step(): return (hidden[None], weight_grad[None], passed_grad[None])]
  transfers between devices with their start and end apart: 3 -> 8, of which waited for: 2 -> 4; matrix products, arithmetic and copies ran while one was open for 15% -> 2% of each run, Pallas kernels for 0% -> 30%
where the time goes in v1:
time: 34.2 us; the launch traced here: 33.9 us
  Pallas kernels  10.1 us (30%)
  starting transfers between devices  7.47 us (22%)
  waiting for transfers between devices  7.47 us (22%)
  local copies, waits for them, and re-layouts  6.7 us (20%)
  other arithmetic  1.51 us (4%)
  between operations  0.68 us (2%)
    pallas_call x4, Pallas kernels, call(): pl.pallas_call(kernel, grid=grid, out_shape=shapes, in_specs=in_specs, ou...  10.1 us
    ppermute x6, waiting for transfers between devices, swapped(): lax.ppermute(value, axis, [(source, source ^ distance) for source in rang...  7.46 us
    unnamed x8, local copies, waits for them, and re-layouts  6.7 us
    ppermute x6, starting transfers between devices, swapped(): lax.ppermute(value, axis, [(source, source ^ distance) for source in rang...  4.88 us
    broadcast_in_dim x2, other arithmetic, paired_step(): return (hidden[None], weight_grad[None], passed_grad[None])  1.51 us
    ppermute x1, starting transfers between devices, shifted(): lax.ppermute(value, axis, [(source, source + steps) for source in range(l...  1.29 us
    ppermute x1, starting transfers between devices, paired_step(): lax.ppermute(crossing, ('section', 'col'), [(section * columns + col, (se...  1.29 us
  transfers between devices with their start and end apart: 8, of which 4 were waited for; matrix products, arithmetic and copies ran while one was open for 2% of the time, Pallas kernels for 30%

profile of v1, /device:TPU:0, one launch (start us, length us, event | category | flops | bytes accessed | tf_op | source)
XLA Modules:
  0.0 33.9 jit_solution(4948184763921727814)
XLA Ops:
  0.6 3.0 %collective-permute-start.4 = (bf16[64,3072]{1,0:T(8,128)(2,1)}, bf16[64,3072]{1,0:T(8,128)(2,1)S(1)}, u32[]{:S(2)}, u32[]{:S(2)}) collective-permute-start(bf16[64,3072]{1,0:T(8,128)(2,1)} %bitcast.10), channel_id=1, source_target_pairs={{0,4},{4,0},{1,5},{5,1},{2,6},{6,2},{3,7},{7,3},{8,12},{12,8},{9,1... | collective-permute-start | bytes 1179656 | tf_op jit(solution)/shard_map/ppermute | solution.py:24
  3.7 1.5 %collective-permute-start.1 = (bf16[32,1536]{1,0:T(8,128)(2,1)}, bf16[32,1536]{1,0:T(8,128)(2,1)S(1)}, u32[]{:S(2)}, u32[]{:S(2)}) collective-permute-start(bf16[32,1536]{1,0:T(8,128)(2,1)} %bitcast.13), channel_id=1, source_target_pairs={{0,2},{1,3},{2,0},{3,1},{4,6},{5,7},{6,4},{7,5},{8,10},{9,11},{10,... | collective-permute-start | bytes 294920 | tf_op jit(solution)/shard_map/ppermute | solution.py:24
  5.2 0.0 collective-permute-start
  5.2 3.3 %collective-permute-done.1.across = bf16[32,1536]{1,0:T(8,128)(2,1)S(1)} collective-permute-done((bf16[32,1536]{1,0:T(8,128)(2,1)}, bf16[32,1536]{1,0:T(8,128)(2,1)S(1)}, u32[]{:S(2)}, u32[]{:S(2)}) %collective-permute-start.1) | collective-permute-done | bytes 98336 | tf_op jit(solution)/shard_map/ppermute | solution.py:24
  8.5 0.0 collective-permute-start.2
  8.5 0.0 collective-permute-done.beside
  8.5 1.3 %collective-permute-done.2.diagonal = bf16[32,1536]{1,0:T(8,128)(2,1)S(1)} collective-permute-done((bf16[32,1536]{1,0:T(8,128)(2,1)S(1)}, bf16[32,1536]{1,0:T(8,128)(2,1)S(1)}, u32[]{:S(2)}, u32[]{:S(2)}) %collective-permute-start.2) | collective-permute-done | bytes 98336 | tf_op jit(solution)/shard_map/ppermute | solution.py:24
  9.8 0.0 copy-start
  9.8 3.7 %copy-done = bf16[1,1536,3072]{2,1,0:T(8,128)(2,1)S(1)} copy-done((bf16[1,1536,3072]{2,1,0:T(8,128)(2,1)S(1)}, bf16[1,1536,3072]{2,1,0:T(8,128)(2,1)}, u32[]{:S(2)}) %copy-start) | copy-done | bytes 9437208
  13.5 0.0 copy-start.3
  13.5 0.9 %copy-done.3 = bf16[1,32,1536]{2,1,0:T(8,128)(2,1)S(1)} copy-done((bf16[1,32,1536]{2,1,0:T(8,128)(2,1)S(1)}, bf16[1,32,1536]{2,1,0:T(8,128)(2,1)}, u32[]{:S(2)}) %copy-start.3) | copy-done | bytes 98328
  14.4 0.0 copy-start.1
  14.4 0.0 copy-start.2
  14.4 1.4 %forward.1 = (bf16[128,1536]{1,0:T(8,128)(2,1)S(1)}, bf16[64,3072]{1,0:T(8,128)(2,1)S(1)}, bf16[64,3072]{1,0:T(8,128)(2,1)S(1)}) custom-call(bf16[32,1536]{1,0:T(8,128)(2,1)S(1)} %bitcast.15, bf16[32,1536]{1,0:T(8,128)(2,1)S(1)} %collective-permute-done.beside, bf16[32,1536]{1,0:T(8,128)(2,1)S(1)} %collective-permute-done.1.across, ...), custom_call_target="tpu_custom_call" | custom-call | flops 1207959552 | bytes 9437184 | tf_op jit(solution)/shard_map/forward/pallas_call | solution.py:52
  15.8 0.1 collective-permute-start.3
  15.9 0.0 collective-permute-done.4.other
  15.9 2.1 %copy-done.1 = bf16[1,1536,3072]{2,1,0:T(8,128)(2,1)S(1)} copy-done((bf16[1,1536,3072]{2,1,0:T(8,128)(2,1)S(1)}, bf16[1,1536,3072]{2,1,0:T(8,128)(2,1)}, u32[]{:S(2)}) %copy-start.1) | copy-done | bytes 9437208
  18.0 0.0 copy-done.2
  18.1 3.3 %input_grad.1 = (bf16[64,1536]{1,0:T(8,128)(2,1)S(1)}, f32[64,1536]{1,0:T(8,128)S(1)}) custom-call(bf16[64,3072]{1,0:T(8,128)(2,1)S(1)} %collective-permute-done.4.other, bf16[64,3072]{1,0:T(8,128)(2,1)S(1)} %bitcast.11, bf16[1536,3072]{1,0:T(8,128)(2,1)S(1)} %bitcast.9), custom_call_target="tpu_custom_call" | custom-call | flops 1207959552 | bytes 9437184 | tf_op jit(solution)/shard_map/input_grad/pallas_call | solution.py:52
  21.3 0.2 collective-permute-start.5
  21.5 1.3 %collective-permute-done.5.received = bf16[64,1536]{1,0:T(8,128)(2,1)S(1)} collective-permute-done((bf16[64,1536]{1,0:T(8,128)(2,1)S(1)}, bf16[64,1536]{1,0:T(8,128)(2,1)S(1)}, u32[]{:S(2)}, u32[]{:S(2)}) %collective-permute-start.5) | collective-permute-done | bytes 196640 | tf_op jit(solution)/shard_map/ppermute | solution.py:24
  22.9 1.3 %collective-permute-start.6 = (bf16[32,1536]{1,0:T(8,128)(2,1)S(1)}, bf16[32,1536]{1,0:T(8,128)(2,1)S(1)}, u32[]{:S(2)}, u32[]{:S(2)}) collective-permute-start(bf16[32,1536]{1,0:T(8,128)(2,1)S(1)} %get-tuple-element.21), channel_id=1, source_target_pairs={{8,0},{16,8},{24,16},{9,1},{17,9},{25,17},{10,2},{18,10},{26,18},{... | collective-permute-start | bytes 294920 | tf_op jit(solution)/shard_map/ppermute | solution.py:19
  24.2 1.3 %collective-permute-start.7 = (bf16[32,1536]{1,0:T(8,128)(2,1)S(1)}, bf16[32,1536]{1,0:T(8,128)(2,1)S(1)}, u32[]{:S(2)}, u32[]{:S(2)}) collective-permute-start(bf16[32,1536]{1,0:T(8,128)(2,1)S(1)} %get-tuple-element.22), channel_id=1, source_target_pairs={{8,2},{9,3},{10,0},{11,1},{16,10},{17,11},{18,8},{19,9},{24,18},{2... | collective-permute-start | bytes 294920 | tf_op jit(solution)/shard_map/ppermute | solution.py:173
  25.5 1.5 %collective-permute-done.3 = bf16[64,3072]{1,0:T(8,128)(2,1)S(1)} collective-permute-done((bf16[64,3072]{1,0:T(8,128)(2,1)S(1)}, bf16[64,3072]{1,0:T(8,128)(2,1)S(1)}, u32[]{:S(2)}, u32[]{:S(2)}) %collective-permute-start.3) | collective-permute-done | bytes 393248 | tf_op jit(solution)/shard_map/ppermute | solution.py:24
  27.0 0.8 %fusion = bf16[1,64,3072]{2,1,0:T(8,128)(2,1)} fusion(bf16[64,3072]{1,0:T(8,128)(2,1)S(1)} %collective-permute-done.3, bf16[64,3072]{1,0:T(8,128)(2,1)S(1)} %get-tuple-element.13), kind=kLoop, calls=%fused_computation.1 | loop fusion | flops 786432 | bytes 1179648 | tf_op jit(solution)/shard_map/broadcast_in_dim | solution.py:200
  27.9 5.4 %weight_grad.1 = bf16[1536,3072]{1,0:T(8,128)(2,1)} custom-call(bf16[128,1536]{1,0:T(8,128)(2,1)S(1)} %get-tuple-element.20.tokens, bf16[64,3072]{1,0:T(8,128)(2,1)S(1)} %collective-permute-done.4.other, bf16[64,3072]{1,0:T(8,128)(2,1)S(1)} %bitcast.12), custom_call_target="tpu_custom_call" | custom-call | flops 1207959552 | bytes 9437184 | tf_op jit(solution)/shard_map/weight_grad/pallas_call | solution.py:52
  33.2 0.0 collective-permute-done.6
  33.2 0.0 collective-permute-done.7
  33.2 0.7 %fusion.1 = bf16[1,32,1536]{2,1,0:T(8,128)(2,1)} fusion(bf16[32,1536]{1,0:T(8,128)(2,1)S(1)} %collective-permute-done.7, bf16[32,1536]{1,0:T(8,128)(2,1)S(1)} %collective-permute-done.6), kind=kLoop, calls=%fused_computation.3 | loop fusion | flops 196608 | bytes 294912 | tf_op jit(solution)/shard_map/broadcast_in_dim | solution.py:200
  (1 shorter events, 0.0 us)
Async XLA Ops:
  0.6 15.3 %collective-permute-start.4 = (bf16[64,3072]{1,0:T(8,128)(2,1)}, bf16[64,3072]{1,0:T(8,128)(2,1)S(1)}, u32[]{:S(2)}, u32[]{:S(2)}) collective-permute-start(bf16[64,3072]{1,0:T(8,128)(2,1)} %bitcast.10), channel_id=1, source_target_pairs={{0,4},{4,0},{1,5},{5,1},{2,6},{6,2},{3,7},{7,3},{8,12},{12,8},{9,1... | collective-permute-start | bytes 1179656 | tf_op jit(solution)/shard_map/ppermute | solution.py:24
  3.7 4.8 %collective-permute-start.1 = (bf16[32,1536]{1,0:T(8,128)(2,1)}, bf16[32,1536]{1,0:T(8,128)(2,1)S(1)}, u32[]{:S(2)}, u32[]{:S(2)}) collective-permute-start(bf16[32,1536]{1,0:T(8,128)(2,1)} %bitcast.13), channel_id=1, source_target_pairs={{0,2},{1,3},{2,0},{3,1},{4,6},{5,7},{6,4},{7,5},{8,10},{9,11},{10,... | collective-permute-start | bytes 294920 | tf_op jit(solution)/shard_map/ppermute | solution.py:24
  5.2 3.3 %collective-permute-start = (bf16[32,1536]{1,0:T(8,128)(2,1)}, bf16[32,1536]{1,0:T(8,128)(2,1)S(1)}, u32[]{:S(2)}, u32[]{:S(2)}) collective-permute-start(bf16[32,1536]{1,0:T(8,128)(2,1)} %bitcast.14), channel_id=1, source_target_pairs={{0,1},{1,0},{2,3},{3,2},{4,5},{5,4},{6,7},{7,6},{8,9},{9,8},{10,11... | collective-permute-start | bytes 294920 | tf_op jit(solution)/shard_map/ppermute | solution.py:24
  8.5 1.3 %collective-permute-start.2 = (bf16[32,1536]{1,0:T(8,128)(2,1)S(1)}, bf16[32,1536]{1,0:T(8,128)(2,1)S(1)}, u32[]{:S(2)}, u32[]{:S(2)}) collective-permute-start(bf16[32,1536]{1,0:T(8,128)(2,1)S(1)} %collective-permute-done.1.across), channel_id=1, source_target_pairs={{0,1},{1,0},{2,3},{3,2},{4,5},{5,4},{6,7},{7,6},{8,9},{9,8},{10,11... | collective-permute-start | bytes 294920 | tf_op jit(solution)/shard_map/ppermute | solution.py:24
  9.8 3.7 %copy-start = (bf16[1,1536,3072]{2,1,0:T(8,128)(2,1)S(1)}, bf16[1,1536,3072]{2,1,0:T(8,128)(2,1)}, u32[]{:S(2)}) copy-start(bf16[1,1536,3072]{2,1,0:T(8,128)(2,1)} %param.4) | copy-start | bytes 28311556
  13.5 0.9 %copy-start.3 = (bf16[1,32,1536]{2,1,0:T(8,128)(2,1)S(1)}, bf16[1,32,1536]{2,1,0:T(8,128)(2,1)}, u32[]{:S(2)}) copy-start(bf16[1,32,1536]{2,1,0:T(8,128)(2,1)} %param.3) | copy-start | bytes 294916
  14.4 3.7 %copy-start.1 = (bf16[1,1536,3072]{2,1,0:T(8,128)(2,1)S(1)}, bf16[1,1536,3072]{2,1,0:T(8,128)(2,1)}, u32[]{:S(2)}) copy-start(bf16[1,1536,3072]{2,1,0:T(8,128)(2,1)} %param.4) | copy-start | bytes 28311556
  14.4 3.7 %copy-start.2 = (bf16[1,64,3072]{2,1,0:T(8,128)(2,1)S(1)}, bf16[1,64,3072]{2,1,0:T(8,128)(2,1)}, u32[]{:S(2)}) copy-start(bf16[1,64,3072]{2,1,0:T(8,128)(2,1)} %param.5) | copy-start | bytes 1179652
  15.8 11.2 %collective-permute-start.3 = (bf16[64,3072]{1,0:T(8,128)(2,1)S(1)}, bf16[64,3072]{1,0:T(8,128)(2,1)S(1)}, u32[]{:S(2)}, u32[]{:S(2)}) collective-permute-start(bf16[64,3072]{1,0:T(8,128)(2,1)S(1)} %get-tuple-element.14), channel_id=1, source_target_pairs={{0,4},{4,0},{1,5},{5,1},{2,6},{6,2},{3,7},{7,3},{8,12},{12,8},{9,1... | collective-permute-start | bytes 1179656 | tf_op jit(solution)/shard_map/ppermute | solution.py:24
  21.3 1.5 %collective-permute-start.5 = (bf16[64,1536]{1,0:T(8,128)(2,1)S(1)}, bf16[64,1536]{1,0:T(8,128)(2,1)S(1)}, u32[]{:S(2)}, u32[]{:S(2)}) collective-permute-start(bf16[64,1536]{1,0:T(8,128)(2,1)S(1)} %get-tuple-element.17), channel_id=1, source_target_pairs={{0,1},{1,0},{2,3},{3,2},{4,5},{5,4},{6,7},{7,6},{8,9},{9,8},{10,11... | collective-permute-start | bytes 589832 | tf_op jit(solution)/shard_map/ppermute | solution.py:24
  22.9 10.3 %collective-permute-start.6 = (bf16[32,1536]{1,0:T(8,128)(2,1)S(1)}, bf16[32,1536]{1,0:T(8,128)(2,1)S(1)}, u32[]{:S(2)}, u32[]{:S(2)}) collective-permute-start(bf16[32,1536]{1,0:T(8,128)(2,1)S(1)} %get-tuple-element.21), channel_id=1, source_target_pairs={{8,0},{16,8},{24,16},{9,1},{17,9},{25,17},{10,2},{18,10},{26,18},{... | collective-permute-start | bytes 294920 | tf_op jit(solution)/shard_map/ppermute | solution.py:19
  24.2 9.0 %collective-permute-start.7 = (bf16[32,1536]{1,0:T(8,128)(2,1)S(1)}, bf16[32,1536]{1,0:T(8,128)(2,1)S(1)}, u32[]{:S(2)}, u32[]{:S(2)}) collective-permute-start(bf16[32,1536]{1,0:T(8,128)(2,1)S(1)} %get-tuple-element.22), channel_id=1, source_target_pairs={{8,2},{9,3},{10,0},{11,1},{16,10},{17,11},{18,8},{19,9},{24,18},{2... | collective-permute-start | bytes 294920 | tf_op jit(solution)/shard_map/ppermute | solution.py:173

commit v2 on v1

--- a/solution.py
+++ b/solution.py
@@ -44,7 +44,7 @@
     return (hidden_sum[None], weight_grad[None], shifted(input_grad, "section", -1)[None])
 
 
-def call(kernel, out_shapes, args, scratch=(), flops=0, moved=0, name=None, grid=(), in_specs=None, out_specs=None):
+def call(kernel, out_shapes, args, scratch=(), flops=0, moved=0, name=None, grid=(), in_specs=None, out_specs=None, limit=16 * MIB):
     single = not isinstance(out_shapes, (list, tuple))
     shapes = [out_shapes] if single else list(out_shapes)
     in_specs = in_specs or [VMEM] * len(args)
@@ -56,7 +56,7 @@
         in_specs=in_specs,
         out_specs=out_specs,
         scratch_shapes=list(scratch),
-        compiler_params=pltpu.CompilerParams(vmem_limit_bytes=16 * MIB),
+        compiler_params=pltpu.CompilerParams(vmem_limit_bytes=limit),
         cost_estimate=pl.CostEstimate(flops=flops, bytes_accessed=moved, transcendentals=0),
         name=name,
     )(*args)
@@ -85,22 +85,33 @@
         keep_out[:, lower : lower + tile] = product[half:]
 
 
-def input_grad_kernel(other, own, weight, send_out, keep_out, total, *, tile):
+def load_kernel(weight, own, grads, weight_out, own_out, grads_out, sems):
+    copies = [
+        pltpu.make_async_copy(source, target, sems.at[index])
+        for index, (source, target) in enumerate(
+            ((own, own_out), (grads, grads_out), (weight, weight_out))
+        )
+    ]
+    for copy in copies:
+        copy.start()
+    for copy in copies:
+        copy.wait()
+
+
+def input_grad_kernel(other, own, weight, send_out, keep_out, *, tile):
     rows = own.shape[0] // 2
     core = lax.axis_index("col") % 2
-    grads = jnp.concatenate([other[...], own[...]], axis=0)
+    mine = pl.multiple_of(core * rows, rows)
+    theirs = pl.multiple_of((1 - core) * rows, rows)
+    grads = jnp.concatenate(
+        [ref[pl.ds(start, rows), :] for start in (theirs, mine) for ref in (other, own)], axis=0
+    ).T
     for lower in range(0, weight.shape[0], tile):
-        total[:, lower : lower + tile] = lax.dot_general(
-            grads,
-            weight[lower : lower + tile, :],
-            (((1,), (1,)), ((), ())),
-            preferred_element_type=F32,
-        )
-    for half in range(2):
-        mine = pl.multiple_of(2 * half * rows + core * rows, rows)
-        theirs = pl.multiple_of(2 * half * rows + (1 - core) * rows, rows)
-        keep_out[half * rows : (half + 1) * rows, :] = total[pl.ds(mine, rows), :]
-        send_out[half * rows : (half + 1) * rows, :] = total[pl.ds(theirs, rows), :].astype(BF16)
+        total = jnp.dot(
+            weight[lower : lower + tile, :], grads, preferred_element_type=F32
+        ).T
+        send_out[:, lower : lower + tile] = total[: 2 * rows].astype(BF16)
+        keep_out[:, lower : lower + tile] = total[2 * rows :]
 
 
 def pair_kernel(keep, received, straight_out, across_out):
@@ -117,11 +128,27 @@
     ).astype(BF16)
 
 
-def weight_grad_kernel(tokens, other, own, out):
-    grads = jnp.concatenate([other[...], own[...]], axis=0)
-    out[...] = lax.dot_general(
-        tokens[...], grads, (((0,), (0,)), ((), ())), preferred_element_type=F32
-    ).astype(BF16)
+def weight_grad_kernel(tokens, other, own, out, turned, blocks, sems, *, tile):
+    turned[...] = tokens[...].T
+    copies = []
+    for index in range(out.shape[1] // tile):
+        lower = index * tile
+        grads = jnp.concatenate(
+            [other[:, lower : lower + tile], own[:, lower : lower + tile]], axis=0
+        )
+        blocks[index] = jnp.dot(turned[...], grads, preferred_element_type=F32).astype(BF16)
+        copy = pltpu.make_async_copy(
+            blocks.at[index], out.at[:, pl.ds(lower, tile)], sems.at[index]
+        )
+        copy.start()
+        copies.append(copy)
+    for copy in copies:
+        copy.wait()
+
+
+def sum_kernel(hidden_keep, hidden_received, straight, crossing, hidden_out, passed_out):
+    hidden_out[...] = (hidden_keep[...].astype(F32) + hidden_received[...].astype(F32)).astype(BF16)
+    passed_out[...] = (straight[...].astype(F32) + crossing[...].astype(F32)).astype(BF16)
 
 
 def paired_step(tokens, weights, hidden_grads):
@@ -133,8 +160,20 @@
     grads_other = swapped(grads, "row", 1)
     across = swapped(own, "col", 2)
     beside = swapped(own, "col", 1)
+    flops = 4 * half * width * units
+    anywhere = pl.BlockSpec(memory_space=pltpu.HBM)
+    weight, own, grads = call(
+        load_kernel,
+        [jax.ShapeDtypeStruct(value.shape, BF16) for value in (weight, own, grads)],
+        [pltpu.with_memory_space_constraint(value, pltpu.HBM) for value in (weight, own, grads)],
+        scratch=[pltpu.SemaphoreType.DMA((3,))],
+        in_specs=[anywhere] * 3,
+        moved=4 * width * units,
+        limit=40 * MIB,
+        name="load",
+    )
+    across, weight = lax.optimization_barrier((across, weight))
     diagonal = swapped(across, "col", 1)
-    flops = 4 * half * width * units
     tokens_all, hidden_send, hidden_keep = call(
         functools.partial(forward_kernel, tile=512),
         [
@@ -155,7 +194,6 @@
             jax.ShapeDtypeStruct((half, width), F32),
         ],
         (grads_other, grads, weight),
-        scratch=[pltpu.VMEM((2 * half, width), F32)],
         flops=flops,
         moved=2 * width * units,
         name="input_grad",
@@ -181,22 +219,26 @@
     )
     block = 512
     weight_grad = call(
-        weight_grad_kernel,
+        functools.partial(weight_grad_kernel, tile=block),
         jax.ShapeDtypeStruct((width, units), BF16),
         (tokens_late, grads_other, grads),
-        grid=(width // block,),
-        in_specs=[
-            pl.BlockSpec((2 * half, block), lambda step: (0, step)),
-            pl.BlockSpec((half, units), lambda step: (0, 0)),
-            pl.BlockSpec((half, units), lambda step: (0, 0)),
-        ],
-        out_specs=[pl.BlockSpec((block, units), lambda step: (step, 0))],
+        scratch=[
+            pltpu.VMEM((width, 2 * half), BF16),
+            pltpu.VMEM((units // block, width, block), BF16),
+            pltpu.SemaphoreType.DMA((units // block,)),
+        ],
+        out_specs=[anywhere],
         flops=flops,
         moved=2 * width * units,
         name="weight_grad",
     )
-    passed_grad = (straight_received.astype(F32) + crossing_received.astype(F32)).astype(BF16)
-    hidden = (hidden_keep.astype(F32) + hidden_received.astype(F32)).astype(BF16)
+    hidden, passed_grad = call(
+        sum_kernel,
+        [jax.ShapeDtypeStruct((half, units), BF16), jax.ShapeDtypeStruct((rows, width), BF16)],
+        (hidden_keep, hidden_received, straight_received, crossing_received),
+        moved=8 * half * units,
+        name="final_sum",
+    )
     return (hidden[None], weight_grad[None], passed_grad[None])
 
 

time: 34.2 us -> 28.3 us (0.83)
  local copies, waits for them, and re-layouts: 6.7 us -> 0 us
  Pallas kernels: 10.1 us -> 13.2 us
  waiting for transfers between devices: 7.47 us -> 5.84 us
  other arithmetic: 1.51 us -> 0 us
  starting transfers between devices: 7.47 us -> 8.33 us
    unnamed x8 -> x0, local copies, waits for them, and re-layouts: 6.7 us -> none
    ppermute x6, waiting for transfers between devices: 7.46 us -> 2.78 us  [swapped(): lax.ppermute(value, axis, [(source, source ^ distance) for source in rang...]
    pallas_call x4 -> x6, Pallas kernels: 10.1 us -> 13.2 us  [call(): pl.pallas_call(kernel, grid=grid, out_shape=shapes, in_specs=in_specs, ou...]
    ppermute x1, waiting for transfers between devices: 0.01 us -> 3.06 us  [paired_step(): lax.ppermute(crossing, ('section', 'col'), [(section * columns + col, (se...]
    broadcast_in_dim x2 -> x0, other arithmetic: 1.51 us -> none  [paired_step(): return (hidden[None], weight_grad[None], passed_grad[None])]
    ppermute x6, starting transfers between devices: 4.88 us -> 5.75 us  [swapped(): lax.ppermute(value, axis, [(source, source ^ distance) for source in rang...]
  transfers between devices with their start and end apart: 8 -> 8, of which waited for: 4 -> 4; matrix products, arithmetic and copies ran while one was open for 2% -> 0% of each run, Pallas kernels for 30% -> 44%
where the time goes in v2:
time: 28.3 us; the launch traced here: 28.1 us
  Pallas kernels  13.2 us (47%)
  starting transfers between devices  8.33 us (29%)
  waiting for transfers between devices  5.84 us (21%)
  between operations  0.71 us (3%)
    pallas_call x6, Pallas kernels, call(): pl.pallas_call(kernel, grid=grid, out_shape=shapes, in_specs=in_specs, ou...  13.2 us
    ppermute x6, starting transfers between devices, swapped(): lax.ppermute(value, axis, [(source, source ^ distance) for source in rang...  5.75 us
    ppermute x1, waiting for transfers between devices, paired_step(): lax.ppermute(crossing, ('section', 'col'), [(section * columns + col, (se...  3.06 us
    ppermute x6, waiting for transfers between devices, swapped(): lax.ppermute(value, axis, [(source, source ^ distance) for source in rang...  2.78 us
    ppermute x1, starting transfers between devices, shifted(): lax.ppermute(value, axis, [(source, source + steps) for source in range(l...  1.29 us
    ppermute x1, starting transfers between devices, paired_step(): lax.ppermute(crossing, ('section', 'col'), [(section * columns + col, (se...  1.29 us
  transfers between devices with their start and end apart: 8, of which 4 were waited for; matrix products, arithmetic and copies ran while one was open for 0% of the time, Pallas kernels for 44%

profile of v2, /device:TPU:0, one launch (start us, length us, event | category | flops | bytes accessed | tf_op | source)
XLA Modules:
  0.0 28.1 jit_solution(18053016805539996457)
XLA Ops:
  0.6 3.0 %collective-permute-start.4 = (bf16[64,3072]{1,0:T(8,128)(2,1)}, bf16[64,3072]{1,0:T(8,128)(2,1)S(1)}, u32[]{:S(2)}, u32[]{:S(2)}) collective-permute-start(bf16[64,3072]{1,0:T(8,128)(2,1)} %bitcast.8), channel_id=1, source_target_pairs={{0,4},{4,0},{1,5},{5,1},{2,6},{6,2},{3,7},{7,3},{8,12},{12,8},{9,1... | collective-permute-start | bytes 1179656 | tf_op jit(solution)/shard_map/ppermute | solution.py:24
  3.7 1.5 %collective-permute-start.1 = (bf16[32,1536]{1,0:T(8,128)(2,1)}, bf16[32,1536]{1,0:T(8,128)(2,1)S(1)}, u32[]{:S(2)}, u32[]{:S(2)}) collective-permute-start(bf16[32,1536]{1,0:T(8,128)(2,1)} %bitcast.10), channel_id=1, source_target_pairs={{0,2},{1,3},{2,0},{3,1},{4,6},{5,7},{6,4},{7,5},{8,10},{9,11},{10,... | collective-permute-start | bytes 294920 | tf_op jit(solution)/shard_map/ppermute | solution.py:24
  5.2 0.0 collective-permute-start
  5.2 3.9 %load.1 = (bf16[1536,3072]{1,0:T(8,128)(2,1)S(1)}, bf16[32,1536]{1,0:T(8,128)(2,1)S(1)}, bf16[64,3072]{1,0:T(8,128)(2,1)S(1)}) custom-call(bf16[1536,3072]{1,0:T(8,128)(2,1)} %bitcast.6, bf16[32,1536]{1,0:T(8,128)(2,1)} %bitcast.12, bf16[64,3072]{1,0:T(8,128)(2,1)} %bitcast.9), custom_call_target="tpu_custom_call" | custom-call | bytes 18874368 | tf_op jit(solution)/shard_map/load/pallas_call | solution.py:52
  9.1 0.0 collective-permute-done.1.across
  9.1 0.6 %collective-permute-start.2 = (bf16[32,1536]{1,0:T(8,128)(2,1)S(1)}, bf16[32,1536]{1,0:T(8,128)(2,1)S(1)}, u32[]{:S(2)}, u32[]{:S(2)}) collective-permute-start(bf16[32,1536]{1,0:T(8,128)(2,1)S(1)} %collective-permute-done.1.across), channel_id=1, source_target_pairs={{0,1},{1,0},{2,3},{3,2},{4,5},{5,4},{6,7},{7,6},{8,9},{9,8},{10,11... | collective-permute-start | bytes 294920 | tf_op jit(solution)/shard_map/ppermute | solution.py:24
  9.6 0.0 collective-permute-done.beside
  9.6 0.9 %collective-permute-done.2.diagonal = bf16[32,1536]{1,0:T(8,128)(2,1)S(1)} collective-permute-done((bf16[32,1536]{1,0:T(8,128)(2,1)S(1)}, bf16[32,1536]{1,0:T(8,128)(2,1)S(1)}, u32[]{:S(2)}, u32[]{:S(2)}) %collective-permute-start.2) | collective-permute-done | bytes 98336 | tf_op jit(solution)/shard_map/ppermute | solution.py:24
  10.6 1.4 %forward.1 = (bf16[128,1536]{1,0:T(8,128)(2,1)S(1)}, bf16[64,3072]{1,0:T(8,128)(2,1)S(1)}, bf16[64,3072]{1,0:T(8,128)(2,1)S(1)}) custom-call(bf16[32,1536]{1,0:T(8,128)(2,1)S(1)} %get-tuple-element.20.own, bf16[32,1536]{1,0:T(8,128)(2,1)S(1)} %collective-permute-done.beside, bf16[32,1536]{1,0:T(8,128)(2,1)S(1)} %collective-permute-done.1.across, ...), custom_call_target="tpu_custom_call" | custom-call | flops 1207959552 | bytes 9437184 | tf_op jit(solution)/shard_map/forward/pallas_call | solution.py:52
  12.0 0.6 %collective-permute-start.3 = (bf16[64,3072]{1,0:T(8,128)(2,1)S(1)}, bf16[64,3072]{1,0:T(8,128)(2,1)S(1)}, u32[]{:S(2)}, u32[]{:S(2)}) collective-permute-start(bf16[64,3072]{1,0:T(8,128)(2,1)S(1)} %get-tuple-element.25), channel_id=1, source_target_pairs={{0,4},{4,0},{1,5},{5,1},{2,6},{6,2},{3,7},{7,3},{8,12},{12,8},{9,1... | collective-permute-start | bytes 1179656 | tf_op jit(solution)/shard_map/ppermute | solution.py:24
  12.6 0.4 %collective-permute-done.4.other = bf16[64,3072]{1,0:T(8,128)(2,1)S(1)} collective-permute-done((bf16[64,3072]{1,0:T(8,128)(2,1)}, bf16[64,3072]{1,0:T(8,128)(2,1)S(1)}, u32[]{:S(2)}, u32[]{:S(2)}) %collective-permute-start.4) | collective-permute-done | bytes 393248 | tf_op jit(solution)/shard_map/ppermute | solution.py:24
  13.0 2.7 %input_grad.1 = (bf16[64,1536]{1,0:T(8,128)(2,1)S(1)}, f32[64,1536]{1,0:T(8,128)S(1)}) custom-call(bf16[64,3072]{1,0:T(8,128)(2,1)S(1)} %collective-permute-done.4.other, bf16[64,3072]{1,0:T(8,128)(2,1)S(1)} %get-tuple-element.27.own, bf16[1536,3072]{1,0:T(8,128)(2,1)S(1)} %get-tuple-element.23.weight), custom_call_target="tpu_custom_call" | custom-call | flops 1207959552 | bytes 9437184 | tf_op jit(solution)/shard_map/input_grad/pallas_call | solution.py:52
  15.7 0.1 collective-permute-start.5
  15.8 1.4 %collective-permute-done.5.received = bf16[64,1536]{1,0:T(8,128)(2,1)S(1)} collective-permute-done((bf16[64,1536]{1,0:T(8,128)(2,1)S(1)}, bf16[64,1536]{1,0:T(8,128)(2,1)S(1)}, u32[]{:S(2)}, u32[]{:S(2)}) %collective-permute-start.5) | collective-permute-done | bytes 196640 | tf_op jit(solution)/shard_map/ppermute | solution.py:24
  17.2 1.3 %collective-permute-start.6 = (bf16[32,1536]{1,0:T(8,128)(2,1)S(1)}, bf16[32,1536]{1,0:T(8,128)(2,1)S(1)}, u32[]{:S(2)}, u32[]{:S(2)}) collective-permute-start(bf16[32,1536]{1,0:T(8,128)(2,1)S(1)} %get-tuple-element.32), channel_id=1, source_target_pairs={{8,0},{16,8},{24,16},{9,1},{17,9},{25,17},{10,2},{18,10},{26,18},{... | collective-permute-start | bytes 294920 | tf_op jit(solution)/shard_map/ppermute | solution.py:19
  18.5 1.3 %collective-permute-start.7 = (bf16[32,1536]{1,0:T(8,128)(2,1)S(1)}, bf16[32,1536]{1,0:T(8,128)(2,1)S(1)}, u32[]{:S(2)}, u32[]{:S(2)}) collective-permute-start(bf16[32,1536]{1,0:T(8,128)(2,1)S(1)} %get-tuple-element.33), channel_id=1, source_target_pairs={{8,2},{9,3},{10,0},{11,1},{16,10},{17,11},{18,8},{19,9},{24,18},{2... | collective-permute-start | bytes 294920 | tf_op jit(solution)/shard_map/ppermute | solution.py:211
  19.8 4.3 %weight_grad.1 = bf16[1536,3072]{1,0:T(8,128)(2,1)} custom-call(bf16[128,1536]{1,0:T(8,128)(2,1)S(1)} %get-tuple-element.35.tokens, bf16[64,3072]{1,0:T(8,128)(2,1)S(1)} %collective-permute-done.4.other, bf16[64,3072]{1,0:T(8,128)(2,1)S(1)} %get-tuple-element.27.own), custom_call_target="tpu_custom_call" | custom-call | flops 1207959552 | bytes 9437184 | tf_op jit(solution)/shard_map/weight_grad/pallas_call | solution.py:52
  24.1 0.0 collective-permute-done.3.hidden_received
  24.2 0.0 collective-permute-done.6.straight
  24.2 3.1 %collective-permute-done.7.crossing = bf16[32,1536]{1,0:T(8,128)(2,1)S(1)} collective-permute-done((bf16[32,1536]{1,0:T(8,128)(2,1)S(1)}, bf16[32,1536]{1,0:T(8,128)(2,1)S(1)}, u32[]{:S(2)}, u32[]{:S(2)}) %collective-permute-start.7) | collective-permute-done | bytes 98336 | tf_op jit(solution)/shard_map/ppermute | solution.py:211
  27.2 0.9 %final_sum.1 = (bf16[64,3072]{1,0:T(8,128)(2,1)}, bf16[32,1536]{1,0:T(8,128)(2,1)}) custom-call(bf16[64,3072]{1,0:T(8,128)(2,1)S(1)} %get-tuple-element.24.hidden_keep, bf16[64,3072]{1,0:T(8,128)(2,1)S(1)} %collective-permute-done.3.hidden_received, bf16[32,1536]{1,0:T(8,128)(2,1)S(1)} %collective-permute-done.6.straight, ...), custom_call_target="tpu_custom_call" | custom-call | bytes 1572864 | tf_op jit(solution)/shard_map/final_sum/pallas_call | solution.py:52
  (1 shorter events, 0.0 us)
Async XLA Ops:
  0.6 12.4 %collective-permute-start.4 = (bf16[64,3072]{1,0:T(8,128)(2,1)}, bf16[64,3072]{1,0:T(8,128)(2,1)S(1)}, u32[]{:S(2)}, u32[]{:S(2)}) collective-permute-start(bf16[64,3072]{1,0:T(8,128)(2,1)} %bitcast.8), channel_id=1, source_target_pairs={{0,4},{4,0},{1,5},{5,1},{2,6},{6,2},{3,7},{7,3},{8,12},{12,8},{9,1... | collective-permute-start | bytes 1179656 | tf_op jit(solution)/shard_map/ppermute | solution.py:24
  3.7 5.4 %collective-permute-start.1 = (bf16[32,1536]{1,0:T(8,128)(2,1)}, bf16[32,1536]{1,0:T(8,128)(2,1)S(1)}, u32[]{:S(2)}, u32[]{:S(2)}) collective-permute-start(bf16[32,1536]{1,0:T(8,128)(2,1)} %bitcast.10), channel_id=1, source_target_pairs={{0,2},{1,3},{2,0},{3,1},{4,6},{5,7},{6,4},{7,5},{8,10},{9,11},{10,... | collective-permute-start | bytes 294920 | tf_op jit(solution)/shard_map/ppermute | solution.py:24
  5.2 4.5 %collective-permute-start = (bf16[32,1536]{1,0:T(8,128)(2,1)}, bf16[32,1536]{1,0:T(8,128)(2,1)S(1)}, u32[]{:S(2)}, u32[]{:S(2)}) collective-permute-start(bf16[32,1536]{1,0:T(8,128)(2,1)} %bitcast.11), channel_id=1, source_target_pairs={{0,1},{1,0},{2,3},{3,2},{4,5},{5,4},{6,7},{7,6},{8,9},{9,8},{10,11... | collective-permute-start | bytes 294920 | tf_op jit(solution)/shard_map/ppermute | solution.py:24
  9.1 1.5 %collective-permute-start.2 = (bf16[32,1536]{1,0:T(8,128)(2,1)S(1)}, bf16[32,1536]{1,0:T(8,128)(2,1)S(1)}, u32[]{:S(2)}, u32[]{:S(2)}) collective-permute-start(bf16[32,1536]{1,0:T(8,128)(2,1)S(1)} %collective-permute-done.1.across), channel_id=1, source_target_pairs={{0,1},{1,0},{2,3},{3,2},{4,5},{5,4},{6,7},{7,6},{8,9},{9,8},{10,11... | collective-permute-start | bytes 294920 | tf_op jit(solution)/shard_map/ppermute | solution.py:24
  12.0 12.1 %collective-permute-start.3 = (bf16[64,3072]{1,0:T(8,128)(2,1)S(1)}, bf16[64,3072]{1,0:T(8,128)(2,1)S(1)}, u32[]{:S(2)}, u32[]{:S(2)}) collective-permute-start(bf16[64,3072]{1,0:T(8,128)(2,1)S(1)} %get-tuple-element.25), channel_id=1, source_target_pairs={{0,4},{4,0},{1,5},{5,1},{2,6},{6,2},{3,7},{7,3},{8,12},{12,8},{9,1... | collective-permute-start | bytes 1179656 | tf_op jit(solution)/shard_map/ppermute | solution.py:24
  15.7 1.5 %collective-permute-start.5 = (bf16[64,1536]{1,0:T(8,128)(2,1)S(1)}, bf16[64,1536]{1,0:T(8,128)(2,1)S(1)}, u32[]{:S(2)}, u32[]{:S(2)}) collective-permute-start(bf16[64,1536]{1,0:T(8,128)(2,1)S(1)} %get-tuple-element.29), channel_id=1, source_target_pairs={{0,1},{1,0},{2,3},{3,2},{4,5},{5,4},{6,7},{7,6},{8,9},{9,8},{10,11... | collective-permute-start | bytes 589832 | tf_op jit(solution)/shard_map/ppermute | solution.py:24
  17.2 6.9 %collective-permute-start.6 = (bf16[32,1536]{1,0:T(8,128)(2,1)S(1)}, bf16[32,1536]{1,0:T(8,128)(2,1)S(1)}, u32[]{:S(2)}, u32[]{:S(2)}) collective-permute-start(bf16[32,1536]{1,0:T(8,128)(2,1)S(1)} %get-tuple-element.32), channel_id=1, source_target_pairs={{8,0},{16,8},{24,16},{9,1},{17,9},{25,17},{10,2},{18,10},{26,18},{... | collective-permute-start | bytes 294920 | tf_op jit(solution)/shard_map/ppermute | solution.py:19
  18.5 8.7 %collective-permute-start.7 = (bf16[32,1536]{1,0:T(8,128)(2,1)S(1)}, bf16[32,1536]{1,0:T(8,128)(2,1)S(1)}, u32[]{:S(2)}, u32[]{:S(2)}) collective-permute-start(bf16[32,1536]{1,0:T(8,128)(2,1)S(1)} %get-tuple-element.33), channel_id=1, source_target_pairs={{8,2},{9,3},{10,0},{11,1},{16,10},{17,11},{18,8},{19,9},{24,18},{2... | collective-permute-start | bytes 294920 | tf_op jit(solution)/shard_map/ppermute | solution.py:211

commit v3 on v2

--- a/solution.py
+++ b/solution.py
@@ -85,33 +85,63 @@
         keep_out[:, lower : lower + tile] = product[half:]
 
 
-def load_kernel(weight, own, grads, weight_out, own_out, grads_out, sems):
-    copies = [
-        pltpu.make_async_copy(source, target, sems.at[index])
-        for index, (source, target) in enumerate(
-            ((own, own_out), (grads, grads_out), (weight, weight_out))
+def turn(weight, out, lower, upper, offset):
+    size = min(256, weight.shape[1])
+    down = lax.broadcasted_iota(jnp.int32, (size, size), 0)
+    right = lax.broadcasted_iota(jnp.int32, (size, size), 1)
+    identity = jnp.where(down == right, 1.0, 0.0).astype(BF16)
+    for unit in range(0, weight.shape[1], size):
+        out[unit : unit + size, lower - offset : upper - offset] = lax.dot_general(
+            identity,
+            weight[lower:upper, unit : unit + size],
+            (((1,), (1,)), ((), ())),
+            preferred_element_type=F32,
+        ).astype(BF16)
+
+
+def load_kernel(weight, own, grads, weight_out, turned_out, own_out, grads_out, sems, *, chunk):
+    small = [
+        pltpu.make_async_copy(own, own_out, sems.at[0]),
+        pltpu.make_async_copy(grads, grads_out, sems.at[1]),
+    ]
+    large = [
+        pltpu.make_async_copy(
+            weight.at[pl.ds(lower, chunk)], weight_out.at[pl.ds(lower, chunk)], sems.at[2 + index]
         )
+        for index, lower in enumerate(range(0, weight.shape[0], chunk))
     ]
-    for copy in copies:
+    for copy in large[:1] + small + large[1:]:
         copy.start()
-    for copy in copies:
+    for index, copy in enumerate(large):
         copy.wait()
-
-
-def input_grad_kernel(other, own, weight, send_out, keep_out, *, tile):
+        if (index + 1) * chunk <= turned_out.shape[1]:
+            turn(weight_out, turned_out, index * chunk, (index + 1) * chunk, 0)
+    for copy in small:
+        copy.wait()
+
+
+def turn_kernel(weight, out, *, chunk):
+    done = weight.shape[0] - out.shape[1]
+    for lower in range(done, weight.shape[0], chunk):
+        turn(weight, out, lower, lower + chunk, done)
+
+
+def input_grad_kernel(other, own, first, second, send_out, keep_out, *, tile):
     rows = own.shape[0] // 2
     core = lax.axis_index("col") % 2
     mine = pl.multiple_of(core * rows, rows)
     theirs = pl.multiple_of((1 - core) * rows, rows)
     grads = jnp.concatenate(
         [ref[pl.ds(start, rows), :] for start in (theirs, mine) for ref in (other, own)], axis=0
-    ).T
-    for lower in range(0, weight.shape[0], tile):
-        total = jnp.dot(
-            weight[lower : lower + tile, :], grads, preferred_element_type=F32
-        ).T
-        send_out[:, lower : lower + tile] = total[: 2 * rows].astype(BF16)
-        keep_out[:, lower : lower + tile] = total[2 * rows :]
+    )
+    offset = 0
+    for turned in (first, second):
+        for lower in range(0, turned.shape[1], tile):
+            total = jnp.dot(grads, turned[:, lower : lower + tile], preferred_element_type=F32)
+            columns = pl.ds(offset + lower, tile)
+            send_out[:, columns] = total[: 2 * rows].astype(BF16)
+            keep_out[:, columns] = total[2 * rows :]
+        offset += turned.shape[1]
 
 
 def pair_kernel(keep, received, straight_out, across_out):
@@ -162,18 +192,32 @@
     beside = swapped(own, "col", 1)
     flops = 4 * half * width * units
     anywhere = pl.BlockSpec(memory_space=pltpu.HBM)
-    weight, own, grads = call(
-        load_kernel,
-        [jax.ShapeDtypeStruct(value.shape, BF16) for value in (weight, own, grads)],
+    chunk = 256
+    early = chunk * 4
+    weight, turned_first, own, grads = call(
+        functools.partial(load_kernel, chunk=chunk),
+        [
+            jax.ShapeDtypeStruct(shape, BF16)
+            for shape in (weight.shape, (units, early), own.shape, grads.shape)
+        ],
         [pltpu.with_memory_space_constraint(value, pltpu.HBM) for value in (weight, own, grads)],
-        scratch=[pltpu.SemaphoreType.DMA((3,))],
+        scratch=[pltpu.SemaphoreType.DMA((2 + width // chunk,))],
         in_specs=[anywhere] * 3,
         moved=4 * width * units,
-        limit=40 * MIB,
+        limit=16 * MIB,
         name="load",
     )
     across, weight = lax.optimization_barrier((across, weight))
     diagonal = swapped(across, "col", 1)
+    turned_second = call(
+        functools.partial(turn_kernel, chunk=chunk),
+        jax.ShapeDtypeStruct((units, width - early), BF16),
+        (weight,),
+        flops=2 * units * (width - early) * chunk,
+        moved=4 * units * (width - early),
+        name="turn",
+    )
+    diagonal, turned_second = lax.optimization_barrier((diagonal, turned_second))
     tokens_all, hidden_send, hidden_keep = call(
         functools.partial(forward_kernel, tile=512),
         [
@@ -193,7 +237,7 @@
             jax.ShapeDtypeStruct((half, width), BF16),
             jax.ShapeDtypeStruct((half, width), F32),
         ],
-        (grads_other, grads, weight),
+        (grads_other, grads, turned_first, turned_second),
         flops=flops,
         moved=2 * width * units,
         name="input_grad",

time: 28.3 us -> 27 us (0.954)
  waiting for transfers between devices: 5.84 us -> 4.78 us
    ppermute x1, waiting for transfers between devices: 3.06 us -> 2.43 us  [paired_step(): lax.ppermute(crossing, ('section', 'col'), [(section * columns + col, (se...]
    ppermute x6, waiting for transfers between devices: 2.78 us -> 2.35 us  [swapped(): lax.ppermute(value, axis, [(source, source ^ distance) for source in rang...]
    pallas_call x6 -> x7, Pallas kernels: 13.2 us -> 13 us  [call(): pl.pallas_call(kernel, grid=grid, out_shape=shapes, in_specs=in_specs, ou...]
  transfers between devices with their start and end apart: 8 -> 8, of which waited for: 4 -> 4; matrix products, arithmetic and copies ran while one was open for 0% -> 0% of each run, Pallas kernels for 44% -> 45%
where the time goes in v3:
time: 27 us; the launch traced here: 26.8 us
  Pallas kernels  13 us (48%)
  starting transfers between devices  8.31 us (31%)
  waiting for transfers between devices  4.78 us (18%)
  between operations  0.75 us (3%)
    pallas_call x7, Pallas kernels, call(): pl.pallas_call(kernel, grid=grid, out_shape=shapes, in_specs=in_specs, ou...  13 us
    ppermute x6, starting transfers between devices, swapped(): lax.ppermute(value, axis, [(source, source ^ distance) for source in rang...  5.73 us
    ppermute x1, waiting for transfers between devices, paired_step(): lax.ppermute(crossing, ('section', 'col'), [(section * columns + col, (se...  2.43 us
    ppermute x6, waiting for transfers between devices, swapped(): lax.ppermute(value, axis, [(source, source ^ distance) for source in rang...  2.35 us
    ppermute x1, starting transfers between devices, shifted(): lax.ppermute(value, axis, [(source, source + steps) for source in range(l...  1.29 us
    ppermute x1, starting transfers between devices, paired_step(): lax.ppermute(crossing, ('section', 'col'), [(section * columns + col, (se...  1.29 us
  transfers between devices with their start and end apart: 8, of which 4 were waited for; matrix products, arithmetic and copies ran while one was open for 0% of the time, Pallas kernels for 45%

profile of v3, /device:TPU:0, one launch (start us, length us, event | category | flops | bytes accessed | tf_op | source)
XLA Modules:
  0.0 26.8 jit_solution(15422135551878441029)
XLA Ops:
  0.6 0.0 copy-start
  0.6 3.0 %collective-permute-start.4 = (bf16[64,3072]{1,0:T(8,128)(2,1)}, bf16[64,3072]{1,0:T(8,128)(2,1)S(1)}, u32[]{:S(2)}, u32[]{:S(2)}) collective-permute-start(bf16[64,3072]{1,0:T(8,128)(2,1)} %bitcast.8), channel_id=1, source_target_pairs={{0,4},{4,0},{1,5},{5,1},{2,6},{6,2},{3,7},{7,3},{8,12},{12,8},{9,1... | collective-permute-start | bytes 1179656 | tf_op jit(solution)/shard_map/ppermute | solution.py:24
  3.7 1.5 %collective-permute-start.1 = (bf16[32,1536]{1,0:T(8,128)(2,1)}, bf16[32,1536]{1,0:T(8,128)(2,1)S(1)}, u32[]{:S(2)}, u32[]{:S(2)}) collective-permute-start(bf16[32,1536]{1,0:T(8,128)(2,1)} %bitcast.10), channel_id=1, source_target_pairs={{0,2},{1,3},{2,0},{3,1},{4,6},{5,7},{6,4},{7,5},{8,10},{9,11},{10,... | collective-permute-start | bytes 294920 | tf_op jit(solution)/shard_map/ppermute | solution.py:24
  5.2 3.9 %load.1 = (bf16[1536,3072]{1,0:T(8,128)(2,1)S(1)}, bf16[3072,1024]{1,0:T(8,128)(2,1)S(1)}, bf16[32,1536]{1,0:T(8,128)(2,1)S(1)}, bf16[64,3072]{1,0:T(8,128)(2,1)S(1)}) custom-call(bf16[1536,3072]{1,0:T(8,128)(2,1)} %bitcast.6, bf16[32,1536]{1,0:T(8,128)(2,1)} %bitcast.11, bf16[64,3072]{1,0:T(8,128)(2,1)} %bitcast.9), custom_call_target="tpu_custom_call" | custom-call | bytes 18874368 | tf_op jit(solution)/shard_map/load/pallas_call | solution.py:52
  9.1 0.0 collective-permute-done.1.across
  9.1 0.1 collective-permute-start.2
  9.2 0.0 copy-done
  9.2 0.5 %collective-permute-start = (bf16[32,1536]{1,0:T(8,128)(2,1)S(1)}, bf16[32,1536]{1,0:T(8,128)(2,1)S(1)}, u32[]{:S(2)}, u32[]{:S(2)}) collective-permute-start(bf16[32,1536]{1,0:T(8,128)(2,1)S(1)} %bitcast.12), channel_id=1, source_target_pairs={{0,1},{1,0},{2,3},{3,2},{4,5},{5,4},{6,7},{7,6},{8,9},{9,8},{10,11... | collective-permute-start | bytes 294920 | tf_op jit(solution)/shard_map/ppermute | solution.py:24
  9.7 1.0 %turn.1.second = bf16[3072,512]{1,0:T(8,128)(2,1)S(1)} custom-call(bf16[1536,3072]{1,0:T(8,128)(2,1)S(1)} %get-tuple-element.26.weight), custom_call_target="tpu_custom_call" | custom-call | flops 805306368 | bytes 6291456 | tf_op jit(solution)/shard_map/turn/pallas_call | solution.py:52
  10.7 0.0 collective-permute-done.2.diagonal
  10.7 0.0 collective-permute-done.beside
  10.7 1.4 %forward.1 = (bf16[128,1536]{1,0:T(8,128)(2,1)S(1)}, bf16[64,3072]{1,0:T(8,128)(2,1)S(1)}, bf16[64,3072]{1,0:T(8,128)(2,1)S(1)}) custom-call(bf16[32,1536]{1,0:T(8,128)(2,1)S(1)} %get-tuple-element.23.own, bf16[32,1536]{1,0:T(8,128)(2,1)S(1)} %collective-permute-done.beside, bf16[32,1536]{1,0:T(8,128)(2,1)S(1)} %collective-permute-done.1.across, ...), custom_call_target="tpu_custom_call" | custom-call | flops 1207959552 | bytes 9437184 | tf_op jit(solution)/shard_map/forward/pallas_call | solution.py:52
  12.2 0.6 %collective-permute-start.3 = (bf16[64,3072]{1,0:T(8,128)(2,1)S(1)}, bf16[64,3072]{1,0:T(8,128)(2,1)S(1)}, u32[]{:S(2)}, u32[]{:S(2)}) collective-permute-start(bf16[64,3072]{1,0:T(8,128)(2,1)S(1)} %get-tuple-element.29), channel_id=1, source_target_pairs={{0,4},{4,0},{1,5},{5,1},{2,6},{6,2},{3,7},{7,3},{8,12},{12,8},{9,1... | collective-permute-start | bytes 1179656 | tf_op jit(solution)/shard_map/ppermute | solution.py:24
  12.7 0.3 collective-permute-done.4.other
  13.0 1.4 %input_grad.1 = (bf16[64,1536]{1,0:T(8,128)(2,1)S(1)}, f32[64,1536]{1,0:T(8,128)S(1)}) custom-call(bf16[64,3072]{1,0:T(8,128)(2,1)S(1)} %collective-permute-done.4.other, bf16[64,3072]{1,0:T(8,128)(2,1)S(1)} %get-tuple-element.31.own, bf16[3072,1024]{1,0:T(8,128)(2,1)S(1)} %get-tuple-element.32.first, bf16[3072,512]{1,0:T(8,128)(2,1)S(1)} %turn.1.second), custom_call_target="tpu_custom_call" | custom-call | flops 1207959552 | bytes 9437184 | tf_op jit(solution)/shard_map/input_grad/pallas_call | solution.py:52
  14.4 0.1 collective-permute-start.5
  14.5 1.4 %collective-permute-done.5.received = bf16[64,1536]{1,0:T(8,128)(2,1)S(1)} collective-permute-done((bf16[64,1536]{1,0:T(8,128)(2,1)S(1)}, bf16[64,1536]{1,0:T(8,128)(2,1)S(1)}, u32[]{:S(2)}, u32[]{:S(2)}) %collective-permute-start.5) | collective-permute-done | bytes 196640 | tf_op jit(solution)/shard_map/ppermute | solution.py:24
  15.9 1.3 %collective-permute-start.6 = (bf16[32,1536]{1,0:T(8,128)(2,1)S(1)}, bf16[32,1536]{1,0:T(8,128)(2,1)S(1)}, u32[]{:S(2)}, u32[]{:S(2)}) collective-permute-start(bf16[32,1536]{1,0:T(8,128)(2,1)S(1)} %get-tuple-element.38), channel_id=1, source_target_pairs={{8,0},{16,8},{24,16},{9,1},{17,9},{25,17},{10,2},{18,10},{26,18},{... | collective-permute-start | bytes 294920 | tf_op jit(solution)/shard_map/ppermute | solution.py:19
  17.2 1.3 %collective-permute-start.7 = (bf16[32,1536]{1,0:T(8,128)(2,1)S(1)}, bf16[32,1536]{1,0:T(8,128)(2,1)S(1)}, u32[]{:S(2)}, u32[]{:S(2)}) collective-permute-start(bf16[32,1536]{1,0:T(8,128)(2,1)S(1)} %get-tuple-element.39), channel_id=1, source_target_pairs={{8,2},{9,3},{10,0},{11,1},{16,10},{17,11},{18,8},{19,9},{24,18},{2... | collective-permute-start | bytes 294920 | tf_op jit(solution)/shard_map/ppermute | solution.py:255
  18.5 4.3 %weight_grad.1 = bf16[1536,3072]{1,0:T(8,128)(2,1)} custom-call(bf16[128,1536]{1,0:T(8,128)(2,1)S(1)} %get-tuple-element.41.tokens, bf16[64,3072]{1,0:T(8,128)(2,1)S(1)} %collective-permute-done.4.other, bf16[64,3072]{1,0:T(8,128)(2,1)S(1)} %get-tuple-element.31.own), custom_call_target="tpu_custom_call" | custom-call | flops 1207959552 | bytes 9437184 | tf_op jit(solution)/shard_map/weight_grad/pallas_call | solution.py:52
  22.9 0.6 %collective-permute-done.3.hidden_received = bf16[64,3072]{1,0:T(8,128)(2,1)S(1)} collective-permute-done((bf16[64,3072]{1,0:T(8,128)(2,1)S(1)}, bf16[64,3072]{1,0:T(8,128)(2,1)S(1)}, u32[]{:S(2)}, u32[]{:S(2)}) %collective-permute-start.3) | collective-permute-done | bytes 393248 | tf_op jit(solution)/shard_map/ppermute | solution.py:24
  23.5 0.0 collective-permute-done.6.straight
  23.5 2.4 %collective-permute-done.7.crossing = bf16[32,1536]{1,0:T(8,128)(2,1)S(1)} collective-permute-done((bf16[32,1536]{1,0:T(8,128)(2,1)S(1)}, bf16[32,1536]{1,0:T(8,128)(2,1)S(1)}, u32[]{:S(2)}, u32[]{:S(2)}) %collective-permute-start.7) | collective-permute-done | bytes 98336 | tf_op jit(solution)/shard_map/ppermute | solution.py:255
  25.9 0.9 %final_sum.1 = (bf16[64,3072]{1,0:T(8,128)(2,1)}, bf16[32,1536]{1,0:T(8,128)(2,1)}) custom-call(bf16[64,3072]{1,0:T(8,128)(2,1)S(1)} %get-tuple-element.28.hidden_keep, bf16[64,3072]{1,0:T(8,128)(2,1)S(1)} %collective-permute-done.3.hidden_received, bf16[32,1536]{1,0:T(8,128)(2,1)S(1)} %collective-permute-done.6.straight, ...), custom_call_target="tpu_custom_call" | custom-call | bytes 1572864 | tf_op jit(solution)/shard_map/final_sum/pallas_call | solution.py:52
  (1 shorter events, 0.0 us)
Async XLA Ops:
  0.6 8.6 %copy-start = (bf16[1,32,1536]{2,1,0:T(8,128)(2,1)S(1)}, bf16[1,32,1536]{2,1,0:T(8,128)(2,1)}, u32[]{:S(2)}) copy-start(bf16[1,32,1536]{2,1,0:T(8,128)(2,1)} %param.3) | copy-start | bytes 294916
  0.6 12.4 %collective-permute-start.4 = (bf16[64,3072]{1,0:T(8,128)(2,1)}, bf16[64,3072]{1,0:T(8,128)(2,1)S(1)}, u32[]{:S(2)}, u32[]{:S(2)}) collective-permute-start(bf16[64,3072]{1,0:T(8,128)(2,1)} %bitcast.8), channel_id=1, source_target_pairs={{0,4},{4,0},{1,5},{5,1},{2,6},{6,2},{3,7},{7,3},{8,12},{12,8},{9,1... | collective-permute-start | bytes 1179656 | tf_op jit(solution)/shard_map/ppermute | solution.py:24
  3.7 5.4 %collective-permute-start.1 = (bf16[32,1536]{1,0:T(8,128)(2,1)}, bf16[32,1536]{1,0:T(8,128)(2,1)S(1)}, u32[]{:S(2)}, u32[]{:S(2)}) collective-permute-start(bf16[32,1536]{1,0:T(8,128)(2,1)} %bitcast.10), channel_id=1, source_target_pairs={{0,2},{1,3},{2,0},{3,1},{4,6},{5,7},{6,4},{7,5},{8,10},{9,11},{10,... | collective-permute-start | bytes 294920 | tf_op jit(solution)/shard_map/ppermute | solution.py:24
  9.1 1.6 %collective-permute-start.2 = (bf16[32,1536]{1,0:T(8,128)(2,1)S(1)}, bf16[32,1536]{1,0:T(8,128)(2,1)S(1)}, u32[]{:S(2)}, u32[]{:S(2)}) collective-permute-start(bf16[32,1536]{1,0:T(8,128)(2,1)S(1)} %collective-permute-done.1.across), channel_id=1, source_target_pairs={{0,1},{1,0},{2,3},{3,2},{4,5},{5,4},{6,7},{7,6},{8,9},{9,8},{10,11... | collective-permute-start | bytes 294920 | tf_op jit(solution)/shard_map/ppermute | solution.py:24
  9.2 1.5 %collective-permute-start = (bf16[32,1536]{1,0:T(8,128)(2,1)S(1)}, bf16[32,1536]{1,0:T(8,128)(2,1)S(1)}, u32[]{:S(2)}, u32[]{:S(2)}) collective-permute-start(bf16[32,1536]{1,0:T(8,128)(2,1)S(1)} %bitcast.12), channel_id=1, source_target_pairs={{0,1},{1,0},{2,3},{3,2},{4,5},{5,4},{6,7},{7,6},{8,9},{9,8},{10,11... | collective-permute-start | bytes 294920 | tf_op jit(solution)/shard_map/ppermute | solution.py:24
  12.2 11.3 %collective-permute-start.3 = (bf16[64,3072]{1,0:T(8,128)(2,1)S(1)}, bf16[64,3072]{1,0:T(8,128)(2,1)S(1)}, u32[]{:S(2)}, u32[]{:S(2)}) collective-permute-start(bf16[64,3072]{1,0:T(8,128)(2,1)S(1)} %get-tuple-element.29), channel_id=1, source_target_pairs={{0,4},{4,0},{1,5},{5,1},{2,6},{6,2},{3,7},{7,3},{8,12},{12,8},{9,1... | collective-permute-start | bytes 1179656 | tf_op jit(solution)/shard_map/ppermute | solution.py:24
  14.4 1.5 %collective-permute-start.5 = (bf16[64,1536]{1,0:T(8,128)(2,1)S(1)}, bf16[64,1536]{1,0:T(8,128)(2,1)S(1)}, u32[]{:S(2)}, u32[]{:S(2)}) collective-permute-start(bf16[64,1536]{1,0:T(8,128)(2,1)S(1)} %get-tuple-element.35), channel_id=1, source_target_pairs={{0,1},{1,0},{2,3},{3,2},{4,5},{5,4},{6,7},{7,6},{8,9},{9,8},{10,11... | collective-permute-start | bytes 589832 | tf_op jit(solution)/shard_map/ppermute | solution.py:24
  15.9 7.6 %collective-permute-start.6 = (bf16[32,1536]{1,0:T(8,128)(2,1)S(1)}, bf16[32,1536]{1,0:T(8,128)(2,1)S(1)}, u32[]{:S(2)}, u32[]{:S(2)}) collective-permute-start(bf16[32,1536]{1,0:T(8,128)(2,1)S(1)} %get-tuple-element.38), channel_id=1, source_target_pairs={{8,0},{16,8},{24,16},{9,1},{17,9},{25,17},{10,2},{18,10},{26,18},{... | collective-permute-start | bytes 294920 | tf_op jit(solution)/shard_map/ppermute | solution.py:19
  17.2 8.7 %collective-permute-start.7 = (bf16[32,1536]{1,0:T(8,128)(2,1)S(1)}, bf16[32,1536]{1,0:T(8,128)(2,1)S(1)}, u32[]{:S(2)}, u32[]{:S(2)}) collective-permute-start(bf16[32,1536]{1,0:T(8,128)(2,1)S(1)} %get-tuple-element.39), channel_id=1, source_target_pairs={{8,2},{9,3},{10,0},{11,1},{16,10},{17,11},{18,8},{19,9},{24,18},{2... | collective-permute-start | bytes 294920 | tf_op jit(solution)/shard_map/ppermute | solution.py:255

commit v4 on v3

--- a/solution.py
+++ b/solution.py
@@ -17,6 +17,20 @@
     count = lax.axis_size(axis)
     leading, last = (max(0, -steps), min(count, count - steps))
     return lax.ppermute(value, axis, [(source, source + steps) for source in range(leading, last)])
+
+
+def paired_sections(value, first, crossing):
+    sections, columns = lax.axis_size("section"), lax.axis_size("col")
+    pairs = []
+    for section in range(sections):
+        partner = section + 1 if (section - first) % 2 == 0 else section - 1
+        for col in range(columns):
+            if 0 <= partner < sections:
+                target = (partner, col ^ 2 if crossing else col)
+            else:
+                target = (section, col ^ 1)
+            pairs.append((section * columns + col, target[0] * columns + target[1]))
+    return lax.ppermute(value, ("section", "col"), pairs)
 
 
 def swapped(value, axis, distance):
@@ -144,18 +158,17 @@
         offset += turned.shape[1]
 
 
-def pair_kernel(keep, received, straight_out, across_out):
+def pair_kernel(keep, received, *outs):
     rows = keep.shape[0] // 2
-    straight = pl.multiple_of(
-        jnp.where(lax.axis_index("col") // 2 == lax.axis_index("row"), rows, 0), rows
-    )
-    across = pl.multiple_of(rows - straight, rows)
-    straight_out[...] = (
-        keep[pl.ds(straight, rows), :] + received[pl.ds(straight, rows), :].astype(F32)
-    ).astype(BF16)
-    across_out[...] = (
-        keep[pl.ds(across, rows), :] + received[pl.ds(across, rows), :].astype(F32)
-    ).astype(BF16)
+    matches = lax.axis_index("col") // 2 == lax.axis_index("row")
+    straight = pl.multiple_of(jnp.where(matches, rows, 0), rows)
+    crossing = pl.multiple_of(rows - straight, rows)
+    for index, start in enumerate((crossing, straight)):
+        total = (
+            keep[pl.ds(start, rows), :] + received[pl.ds(start, rows), :].astype(F32)
+        ).astype(BF16)
+        for out in outs[index::2]:
+            out[...] = total
 
 
 def weight_grad_kernel(tokens, other, own, out, turned, blocks, sems, *, tile):
@@ -176,17 +189,23 @@
         copy.wait()
 
 
-def sum_kernel(hidden_keep, hidden_received, straight, crossing, hidden_out, passed_out):
+def sum_kernel(hidden_keep, hidden_received, *refs):
+    *received, hidden_out, passed_out = refs
     hidden_out[...] = (hidden_keep[...].astype(F32) + hidden_received[...].astype(F32)).astype(BF16)
-    passed_out[...] = (straight[...].astype(F32) + crossing[...].astype(F32)).astype(BF16)
+    sums = [
+        received[index][...].astype(F32) + received[index + 1][...].astype(F32)
+        for index in (0, 2)
+    ]
+    section = lax.axis_index("section")
+    last = section == lax.axis_size("section") - 1
+    passed = jnp.where(section % 2 == 0, sums[0], sums[1])
+    passed_out[...] = jnp.where(last, jnp.zeros_like(passed), passed).astype(BF16)
 
 
 def paired_step(tokens, weights, hidden_grads):
     own, weight, grads = tokens[0], weights[0], hidden_grads[0]
     rows, width = own.shape
     half, units = grads.shape
-    sections = lax.axis_size("section")
-    columns = lax.axis_size("col")
     grads_other = swapped(grads, "row", 1)
     across = swapped(own, "col", 2)
     beside = swapped(own, "col", 1)
@@ -243,24 +262,17 @@
         name="input_grad",
     )
     piece_received = swapped(piece_send, "col", 1)
-    straight, crossing = call(
+    pieces = call(
         pair_kernel,
-        [jax.ShapeDtypeStruct((rows, width), BF16)] * 2,
+        [jax.ShapeDtypeStruct((rows, width), BF16)] * 4,
         (piece_keep, piece_received),
         moved=8 * half * width,
         name="pair_sum",
     )
-    tokens_late, straight, crossing = lax.optimization_barrier((tokens_all, straight, crossing))
-    straight_received = shifted(straight, "section", -1)
-    crossing_received = lax.ppermute(
-        crossing,
-        ("section", "col"),
-        [
-            (section * columns + col, (section - 1) * columns + (col ^ 2))
-            for section in range(1, sections)
-            for col in range(columns)
-        ],
-    )
+    tokens_late, *pieces = lax.optimization_barrier((tokens_all, *pieces))
+    received = [
+        paired_sections(piece, index // 2, index % 2 == 0) for index, piece in enumerate(pieces)
+    ]
     block = 512
     weight_grad = call(
         functools.partial(weight_grad_kernel, tile=block),
@@ -279,7 +291,7 @@
     hidden, passed_grad = call(
         sum_kernel,
         [jax.ShapeDtypeStruct((half, units), BF16), jax.ShapeDtypeStruct((rows, width), BF16)],
-        (hidden_keep, hidden_received, straight_received, crossing_received),
+        [hidden_keep, hidden_received] + received,
         moved=8 * half * units,
         name="final_sum",
     )

time: 27 us -> 25.4 us (0.941)
  waiting for transfers between devices: 4.78 us -> 1.79 us
  starting transfers between devices: 8.31 us -> 9.48 us
    ppermute x2 -> x4, waiting for transfers between devices: 2.43 us -> 0.09 us  [paired_sections(): return lax.ppermute(value, ('section', 'col'), pairs)]
    ppermute x2 -> x4, starting transfers between devices: 2.58 us -> 3.75 us  [paired_sections(): return lax.ppermute(value, ('section', 'col'), pairs)]
    ppermute x6, waiting for transfers between devices: 2.35 us -> 1.71 us  [swapped(): lax.ppermute(value, axis, [(source, source ^ distance) for source in rang...]
  transfers between devices with their start and end apart: 8 -> 10, of which waited for: 4 -> 3; matrix products, arithmetic and copies ran while one was open for 0% -> 0% of each run, Pallas kernels for 45% -> 48%
where the time goes in v4:
time: 25.4 us; the launch traced here: 25 us
  Pallas kernels  12.9 us (51%)
  starting transfers between devices  9.48 us (37%)
  waiting for transfers between devices  1.79 us (7%)
  between operations  0.75 us (3%)
    pallas_call x7, Pallas kernels, call(): pl.pallas_call(kernel, grid=grid, out_shape=shapes, in_specs=in_specs, ou...  12.9 us
    ppermute x6, starting transfers between devices, swapped(): lax.ppermute(value, axis, [(source, source ^ distance) for source in rang...  5.73 us
    ppermute x4, starting transfers between devices, paired_sections(): return lax.ppermute(value, ('section', 'col'), pairs)  3.75 us
    ppermute x6, waiting for transfers between devices, swapped(): lax.ppermute(value, axis, [(source, source ^ distance) for source in rang...  1.71 us
  transfers between devices with their start and end apart: 10, of which 3 were waited for; matrix products, arithmetic and copies ran while one was open for 0% of the time, Pallas kernels for 48%

profile of v4, /device:TPU:0, one launch (start us, length us, event | category | flops | bytes accessed | tf_op | source)
XLA Modules:
  0.0 25.0 jit_solution(14707424101806732284)
XLA Ops:
  0.6 0.0 copy-start
  0.6 3.0 %collective-permute-start.4 = (bf16[64,3072]{1,0:T(8,128)(2,1)}, bf16[64,3072]{1,0:T(8,128)(2,1)S(1)}, u32[]{:S(2)}, u32[]{:S(2)}) collective-permute-start(bf16[64,3072]{1,0:T(8,128)(2,1)} %bitcast.8), channel_id=1, source_target_pairs={{0,4},{4,0},{1,5},{5,1},{2,6},{6,2},{3,7},{7,3},{8,12},{12,8},{9,1... | collective-permute-start | bytes 1179656 | tf_op jit(solution)/shard_map/ppermute | solution.py:38
  3.7 1.5 %collective-permute-start.1 = (bf16[32,1536]{1,0:T(8,128)(2,1)}, bf16[32,1536]{1,0:T(8,128)(2,1)S(1)}, u32[]{:S(2)}, u32[]{:S(2)}) collective-permute-start(bf16[32,1536]{1,0:T(8,128)(2,1)} %bitcast.10), channel_id=1, source_target_pairs={{0,2},{1,3},{2,0},{3,1},{4,6},{5,7},{6,4},{7,5},{8,10},{9,11},{10,... | collective-permute-start | bytes 294920 | tf_op jit(solution)/shard_map/ppermute | solution.py:38
  5.2 3.9 %load.1 = (bf16[1536,3072]{1,0:T(8,128)(2,1)S(1)}, bf16[3072,1024]{1,0:T(8,128)(2,1)S(1)}, bf16[32,1536]{1,0:T(8,128)(2,1)S(1)}, bf16[64,3072]{1,0:T(8,128)(2,1)S(1)}) custom-call(bf16[1536,3072]{1,0:T(8,128)(2,1)} %bitcast.6, bf16[32,1536]{1,0:T(8,128)(2,1)} %bitcast.11, bf16[64,3072]{1,0:T(8,128)(2,1)} %bitcast.9), custom_call_target="tpu_custom_call" | custom-call | bytes 18874368 | tf_op jit(solution)/shard_map/load/pallas_call | solution.py:66
  9.1 0.0 collective-permute-done.1.across
  9.1 0.1 collective-permute-start.2
  9.2 0.0 copy-done
  9.2 0.5 %collective-permute-start = (bf16[32,1536]{1,0:T(8,128)(2,1)S(1)}, bf16[32,1536]{1,0:T(8,128)(2,1)S(1)}, u32[]{:S(2)}, u32[]{:S(2)}) collective-permute-start(bf16[32,1536]{1,0:T(8,128)(2,1)S(1)} %bitcast.12), channel_id=1, source_target_pairs={{0,1},{1,0},{2,3},{3,2},{4,5},{5,4},{6,7},{7,6},{8,9},{9,8},{10,11... | collective-permute-start | bytes 294920 | tf_op jit(solution)/shard_map/ppermute | solution.py:38
  9.7 1.0 %turn.1.second = bf16[3072,512]{1,0:T(8,128)(2,1)S(1)} custom-call(bf16[1536,3072]{1,0:T(8,128)(2,1)S(1)} %get-tuple-element.30.weight), custom_call_target="tpu_custom_call" | custom-call | flops 805306368 | bytes 6291456 | tf_op jit(solution)/shard_map/turn/pallas_call | solution.py:66
  10.7 0.0 collective-permute-done.2.diagonal
  10.7 0.0 collective-permute-done.beside
  10.7 1.4 %forward.1 = (bf16[128,1536]{1,0:T(8,128)(2,1)S(1)}, bf16[64,3072]{1,0:T(8,128)(2,1)S(1)}, bf16[64,3072]{1,0:T(8,128)(2,1)S(1)}) custom-call(bf16[32,1536]{1,0:T(8,128)(2,1)S(1)} %get-tuple-element.27.own, bf16[32,1536]{1,0:T(8,128)(2,1)S(1)} %collective-permute-done.beside, bf16[32,1536]{1,0:T(8,128)(2,1)S(1)} %collective-permute-done.1.across, ...), custom_call_target="tpu_custom_call" | custom-call | flops 1207959552 | bytes 9437184 | tf_op jit(solution)/shard_map/forward/pallas_call | solution.py:66
  12.2 0.6 %collective-permute-start.3 = (bf16[64,3072]{1,0:T(8,128)(2,1)S(1)}, bf16[64,3072]{1,0:T(8,128)(2,1)S(1)}, u32[]{:S(2)}, u32[]{:S(2)}) collective-permute-start(bf16[64,3072]{1,0:T(8,128)(2,1)S(1)} %get-tuple-element.33), channel_id=1, source_target_pairs={{0,4},{4,0},{1,5},{5,1},{2,6},{6,2},{3,7},{7,3},{8,12},{12,8},{9,1... | collective-permute-start | bytes 1179656 | tf_op jit(solution)/shard_map/ppermute | solution.py:38
  12.7 0.3 %collective-permute-done.4.other = bf16[64,3072]{1,0:T(8,128)(2,1)S(1)} collective-permute-done((bf16[64,3072]{1,0:T(8,128)(2,1)}, bf16[64,3072]{1,0:T(8,128)(2,1)S(1)}, u32[]{:S(2)}, u32[]{:S(2)}) %collective-permute-start.4) | collective-permute-done | bytes 393248 | tf_op jit(solution)/shard_map/ppermute | solution.py:38
  13.0 1.4 %input_grad.1 = (bf16[64,1536]{1,0:T(8,128)(2,1)S(1)}, f32[64,1536]{1,0:T(8,128)S(1)}) custom-call(bf16[64,3072]{1,0:T(8,128)(2,1)S(1)} %collective-permute-done.4.other, bf16[64,3072]{1,0:T(8,128)(2,1)S(1)} %get-tuple-element.35.own, bf16[3072,1024]{1,0:T(8,128)(2,1)S(1)} %get-tuple-element.36.first, bf16[3072,512]{1,0:T(8,128)(2,1)S(1)} %turn.1.second), custom_call_target="tpu_custom_call" | custom-call | flops 1207959552 | bytes 9437184 | tf_op jit(solution)/shard_map/input_grad/pallas_call | solution.py:66
  14.4 0.1 collective-permute-start.5
  14.5 1.4 %collective-permute-done.5.received = bf16[64,1536]{1,0:T(8,128)(2,1)S(1)} collective-permute-done((bf16[64,1536]{1,0:T(8,128)(2,1)S(1)}, bf16[64,1536]{1,0:T(8,128)(2,1)S(1)}, u32[]{:S(2)}, u32[]{:S(2)}) %collective-permute-start.5) | collective-permute-done | bytes 196640 | tf_op jit(solution)/shard_map/ppermute | solution.py:38
  15.9 2.8 %collective-permute-start.6 = (bf16[32,1536]{1,0:T(8,128)(2,1)S(1)}, bf16[32,1536]{1,0:T(8,128)(2,1)S(1)}, u32[]{:S(2)}, u32[]{:S(2)}) collective-permute-start(bf16[32,1536]{1,0:T(8,128)(2,1)S(1)} %get-tuple-element.44), channel_id=1, source_target_pairs={{0,10},{1,11},{2,8},{3,9},{8,2},{9,3},{10,0},{11,1},{16,26},{17,27... | collective-permute-start | bytes 294920 | tf_op jit(solution)/shard_map/ppermute | solution.py:33
  18.7 0.4 %collective-permute-start.7 = (bf16[32,1536]{1,0:T(8,128)(2,1)S(1)}, bf16[32,1536]{1,0:T(8,128)(2,1)S(1)}, u32[]{:S(2)}, u32[]{:S(2)}) collective-permute-start(bf16[32,1536]{1,0:T(8,128)(2,1)S(1)} %get-tuple-element.45), channel_id=1, source_target_pairs={{0,8},{1,9},{2,10},{3,11},{8,0},{9,1},{10,2},{11,3},{16,24},{17,25... | collective-permute-start | bytes 294920 | tf_op jit(solution)/shard_map/ppermute | solution.py:33
  19.2 0.0 collective-permute-start.8
  19.2 0.5 %collective-permute-start.9 = (bf16[32,1536]{1,0:T(8,128)(2,1)S(1)}, bf16[32,1536]{1,0:T(8,128)(2,1)S(1)}, u32[]{:S(2)}, u32[]{:S(2)}) collective-permute-start(bf16[32,1536]{1,0:T(8,128)(2,1)S(1)} %get-tuple-element.47), channel_id=1, source_target_pairs={{0,1},{1,0},{2,3},{3,2},{8,16},{9,17},{10,18},{11,19},{16,8},{17,9... | collective-permute-start | bytes 294920 | tf_op jit(solution)/shard_map/ppermute | solution.py:33
  19.7 4.3 %weight_grad.1 = bf16[1536,3072]{1,0:T(8,128)(2,1)} custom-call(bf16[128,1536]{1,0:T(8,128)(2,1)S(1)} %get-tuple-element.49.tokens, bf16[64,3072]{1,0:T(8,128)(2,1)S(1)} %collective-permute-done.4.other, bf16[64,3072]{1,0:T(8,128)(2,1)S(1)} %get-tuple-element.35.own), custom_call_target="tpu_custom_call" | custom-call | flops 1207959552 | bytes 9437184 | tf_op jit(solution)/shard_map/weight_grad/pallas_call | solution.py:66
  24.0 0.0 collective-permute-done.3.hidden_received
  24.0 0.0 collective-permute-done.6.refs_0_
  24.0 0.1 collective-permute-done.7.refs_1_
  24.1 0.0 collective-permute-done.8.refs_2_
  24.1 0.0 collective-permute-done.9.refs_3_
  24.1 0.9 %final_sum.1 = (bf16[64,3072]{1,0:T(8,128)(2,1)}, bf16[32,1536]{1,0:T(8,128)(2,1)}) custom-call(bf16[64,3072]{1,0:T(8,128)(2,1)S(1)} %get-tuple-element.32.hidden_keep, bf16[64,3072]{1,0:T(8,128)(2,1)S(1)} %collective-permute-done.3.hidden_received, bf16[32,1536]{1,0:T(8,128)(2,1)S(1)} %collective-permute-done.6.refs_0_, ...), custom_call_target="tpu_custom_call" | custom-call | bytes 1572864 | tf_op jit(solution)/shard_map/final_sum/pallas_call | solution.py:66
  (1 shorter events, 0.0 us)
Async XLA Ops:
  0.6 8.6 %copy-start = (bf16[1,32,1536]{2,1,0:T(8,128)(2,1)S(1)}, bf16[1,32,1536]{2,1,0:T(8,128)(2,1)}, u32[]{:S(2)}) copy-start(bf16[1,32,1536]{2,1,0:T(8,128)(2,1)} %param.3) | copy-start | bytes 294916
  0.6 12.4 %collective-permute-start.4 = (bf16[64,3072]{1,0:T(8,128)(2,1)}, bf16[64,3072]{1,0:T(8,128)(2,1)S(1)}, u32[]{:S(2)}, u32[]{:S(2)}) collective-permute-start(bf16[64,3072]{1,0:T(8,128)(2,1)} %bitcast.8), channel_id=1, source_target_pairs={{0,4},{4,0},{1,5},{5,1},{2,6},{6,2},{3,7},{7,3},{8,12},{12,8},{9,1... | collective-permute-start | bytes 1179656 | tf_op jit(solution)/shard_map/ppermute | solution.py:38
  3.7 5.4 %collective-permute-start.1 = (bf16[32,1536]{1,0:T(8,128)(2,1)}, bf16[32,1536]{1,0:T(8,128)(2,1)S(1)}, u32[]{:S(2)}, u32[]{:S(2)}) collective-permute-start(bf16[32,1536]{1,0:T(8,128)(2,1)} %bitcast.10), channel_id=1, source_target_pairs={{0,2},{1,3},{2,0},{3,1},{4,6},{5,7},{6,4},{7,5},{8,10},{9,11},{10,... | collective-permute-start | bytes 294920 | tf_op jit(solution)/shard_map/ppermute | solution.py:38
  9.1 1.6 %collective-permute-start.2 = (bf16[32,1536]{1,0:T(8,128)(2,1)S(1)}, bf16[32,1536]{1,0:T(8,128)(2,1)S(1)}, u32[]{:S(2)}, u32[]{:S(2)}) collective-permute-start(bf16[32,1536]{1,0:T(8,128)(2,1)S(1)} %collective-permute-done.1.across), channel_id=1, source_target_pairs={{0,1},{1,0},{2,3},{3,2},{4,5},{5,4},{6,7},{7,6},{8,9},{9,8},{10,11... | collective-permute-start | bytes 294920 | tf_op jit(solution)/shard_map/ppermute | solution.py:38
  9.2 1.5 %collective-permute-start = (bf16[32,1536]{1,0:T(8,128)(2,1)S(1)}, bf16[32,1536]{1,0:T(8,128)(2,1)S(1)}, u32[]{:S(2)}, u32[]{:S(2)}) collective-permute-start(bf16[32,1536]{1,0:T(8,128)(2,1)S(1)} %bitcast.12), channel_id=1, source_target_pairs={{0,1},{1,0},{2,3},{3,2},{4,5},{5,4},{6,7},{7,6},{8,9},{9,8},{10,11... | collective-permute-start | bytes 294920 | tf_op jit(solution)/shard_map/ppermute | solution.py:38
  12.2 11.8 %collective-permute-start.3 = (bf16[64,3072]{1,0:T(8,128)(2,1)S(1)}, bf16[64,3072]{1,0:T(8,128)(2,1)S(1)}, u32[]{:S(2)}, u32[]{:S(2)}) collective-permute-start(bf16[64,3072]{1,0:T(8,128)(2,1)S(1)} %get-tuple-element.33), channel_id=1, source_target_pairs={{0,4},{4,0},{1,5},{5,1},{2,6},{6,2},{3,7},{7,3},{8,12},{12,8},{9,1... | collective-permute-start | bytes 1179656 | tf_op jit(solution)/shard_map/ppermute | solution.py:38
  14.4 1.5 %collective-permute-start.5 = (bf16[64,1536]{1,0:T(8,128)(2,1)S(1)}, bf16[64,1536]{1,0:T(8,128)(2,1)S(1)}, u32[]{:S(2)}, u32[]{:S(2)}) collective-permute-start(bf16[64,1536]{1,0:T(8,128)(2,1)S(1)} %get-tuple-element.39), channel_id=1, source_target_pairs={{0,1},{1,0},{2,3},{3,2},{4,5},{5,4},{6,7},{7,6},{8,9},{9,8},{10,11... | collective-permute-start | bytes 589832 | tf_op jit(solution)/shard_map/ppermute | solution.py:38
  15.9 8.1 %collective-permute-start.6 = (bf16[32,1536]{1,0:T(8,128)(2,1)S(1)}, bf16[32,1536]{1,0:T(8,128)(2,1)S(1)}, u32[]{:S(2)}, u32[]{:S(2)}) collective-permute-start(bf16[32,1536]{1,0:T(8,128)(2,1)S(1)} %get-tuple-element.44), channel_id=1, source_target_pairs={{0,10},{1,11},{2,8},{3,9},{8,2},{9,3},{10,0},{11,1},{16,26},{17,27... | collective-permute-start | bytes 294920 | tf_op jit(solution)/shard_map/ppermute | solution.py:33
  18.7 5.4 %collective-permute-start.7 = (bf16[32,1536]{1,0:T(8,128)(2,1)S(1)}, bf16[32,1536]{1,0:T(8,128)(2,1)S(1)}, u32[]{:S(2)}, u32[]{:S(2)}) collective-permute-start(bf16[32,1536]{1,0:T(8,128)(2,1)S(1)} %get-tuple-element.45), channel_id=1, source_target_pairs={{0,8},{1,9},{2,10},{3,11},{8,0},{9,1},{10,2},{11,3},{16,24},{17,25... | collective-permute-start | bytes 294920 | tf_op jit(solution)/shard_map/ppermute | solution.py:33
  19.2 4.9 %collective-permute-start.8 = (bf16[32,1536]{1,0:T(8,128)(2,1)S(1)}, bf16[32,1536]{1,0:T(8,128)(2,1)S(1)}, u32[]{:S(2)}, u32[]{:S(2)}) collective-permute-start(bf16[32,1536]{1,0:T(8,128)(2,1)S(1)} %get-tuple-element.46), channel_id=1, source_target_pairs={{0,1},{1,0},{2,3},{3,2},{8,18},{9,19},{10,16},{11,17},{16,10},{17,... | collective-permute-start | bytes 294920 | tf_op jit(solution)/shard_map/ppermute | solution.py:33
  19.2 4.9 %collective-permute-start.9 = (bf16[32,1536]{1,0:T(8,128)(2,1)S(1)}, bf16[32,1536]{1,0:T(8,128)(2,1)S(1)}, u32[]{:S(2)}, u32[]{:S(2)}) collective-permute-start(bf16[32,1536]{1,0:T(8,128)(2,1)S(1)} %get-tuple-element.47), channel_id=1, source_target_pairs={{0,1},{1,0},{2,3},{3,2},{8,16},{9,17},{10,18},{11,19},{16,8},{17,9... | collective-permute-start | bytes 294920 | tf_op jit(solution)/shard_map/ppermute | solution.py:33

commit v5 on v4

--- a/solution.py
+++ b/solution.py
@@ -58,7 +58,7 @@
     return (hidden_sum[None], weight_grad[None], shifted(input_grad, "section", -1)[None])
 
 
-def call(kernel, out_shapes, args, scratch=(), flops=0, moved=0, name=None, grid=(), in_specs=None, out_specs=None, limit=16 * MIB):
+def call(kernel, out_shapes, args, scratch=(), flops=0, moved=0, name=None, grid=(), in_specs=None, out_specs=None, limit=16 * MIB, aliases={}):
     single = not isinstance(out_shapes, (list, tuple))
     shapes = [out_shapes] if single else list(out_shapes)
     in_specs = in_specs or [VMEM] * len(args)
@@ -70,6 +70,7 @@
         in_specs=in_specs,
         out_specs=out_specs,
         scratch_shapes=list(scratch),
+        input_output_aliases=aliases,
         compiler_params=pltpu.CompilerParams(vmem_limit_bytes=limit),
         cost_estimate=pl.CostEstimate(flops=flops, bytes_accessed=moved, transcendentals=0),
         name=name,
@@ -180,18 +181,32 @@
             [other[:, lower : lower + tile], own[:, lower : lower + tile]], axis=0
         )
         blocks[index] = jnp.dot(turned[...], grads, preferred_element_type=F32).astype(BF16)
-        copy = pltpu.make_async_copy(
-            blocks.at[index], out.at[:, pl.ds(lower, tile)], sems.at[index]
-        )
-        copy.start()
-        copies.append(copy)
+        rows = out.shape[0] // 2
+        for part in range(2):
+            copy = pltpu.make_async_copy(
+                blocks.at[index, pl.ds(part * rows, rows)],
+                out.at[pl.ds(part * rows, rows), pl.ds(lower, tile)],
+                sems.at[2 * index + part],
+            )
+            copy.start(priority=part)
+            copies.append(copy)
     for copy in copies:
         copy.wait()
 
 
 def sum_kernel(hidden_keep, hidden_received, *refs):
-    *received, hidden_out, passed_out = refs
-    hidden_out[...] = (hidden_keep[...].astype(F32) + hidden_received[...].astype(F32)).astype(BF16)
+    *received, hidden_out, passed_out, hidden_held, passed_held, sems = refs
+    copies = []
+    rows = hidden_keep.shape[0] // 2
+    for index in range(2):
+        part = pl.ds(index * rows, rows)
+        hidden_held[part, :] = (
+            hidden_keep[part, :].astype(F32) + hidden_received[part, :].astype(F32)
+        ).astype(BF16)
+        copies.append(
+            pltpu.make_async_copy(hidden_held.at[part], hidden_out.at[part], sems.at[index])
+        )
+        copies[-1].start()
     sums = [
         received[index][...].astype(F32) + received[index + 1][...].astype(F32)
         for index in (0, 2)
@@ -199,7 +214,11 @@
     section = lax.axis_index("section")
     last = section == lax.axis_size("section") - 1
     passed = jnp.where(section % 2 == 0, sums[0], sums[1])
-    passed_out[...] = jnp.where(last, jnp.zeros_like(passed), passed).astype(BF16)
+    passed_held[...] = jnp.where(last, jnp.zeros_like(passed), passed).astype(BF16)
+    copies.append(pltpu.make_async_copy(passed_held, passed_out, sems.at[2]))
+    copies[-1].start()
+    for copy in copies:
+        copy.wait()
 
 
 def paired_step(tokens, weights, hidden_grads):
@@ -281,7 +300,7 @@
         scratch=[
             pltpu.VMEM((width, 2 * half), BF16),
             pltpu.VMEM((units // block, width, block), BF16),
-            pltpu.SemaphoreType.DMA((units // block,)),
+            pltpu.SemaphoreType.DMA((2 * units // block,)),
         ],
         out_specs=[anywhere],
         flops=flops,
@@ -292,6 +311,12 @@
         sum_kernel,
         [jax.ShapeDtypeStruct((half, units), BF16), jax.ShapeDtypeStruct((rows, width), BF16)],
         [hidden_keep, hidden_received] + received,
+        scratch=[
+            pltpu.VMEM((half, units), BF16),
+            pltpu.VMEM((rows, width), BF16),
+            pltpu.SemaphoreType.DMA((3,)),
+        ],
+        out_specs=[anywhere] * 2,
         moved=8 * half * units,
         name="final_sum",
     )

time: 25.4 us -> 25.3 us (level)
  no operation moved by 1% of the time
where the time goes in v5:
time: 25.3 us; the launch traced here: 25 us
  Pallas kernels  13 us (51%)
  starting transfers between devices  9.48 us (37%)
  waiting for transfers between devices  1.77 us (7%)
  between operations  0.75 us (3%)
    pallas_call x7, Pallas kernels, call(): pl.pallas_call(kernel, grid=grid, out_shape=shapes, in_specs=in_specs, ou...  13 us
    ppermute x6, starting transfers between devices, swapped(): lax.ppermute(value, axis, [(source, source ^ distance) for source in rang...  5.73 us
    ppermute x4, starting transfers between devices, paired_sections(): return lax.ppermute(value, ('section', 'col'), pairs)  3.75 us
    ppermute x6, waiting for transfers between devices, swapped(): lax.ppermute(value, axis, [(source, source ^ distance) for source in rang...  1.71 us
  transfers between devices with their start and end apart: 10, of which 3 were waited for; matrix products, arithmetic and copies ran while one was open for 0% of the time, Pallas kernels for 48%

profile of v5, /device:TPU:0, one launch (start us, length us, event | category | flops | bytes accessed | tf_op | source)
XLA Modules:
  0.0 25.0 jit_solution(2873824742373021973)
XLA Ops:
  0.6 0.0 copy-start
  0.6 3.0 %collective-permute-start.4 = (bf16[64,3072]{1,0:T(8,128)(2,1)}, bf16[64,3072]{1,0:T(8,128)(2,1)S(1)}, u32[]{:S(2)}, u32[]{:S(2)}) collective-permute-start(bf16[64,3072]{1,0:T(8,128)(2,1)} %bitcast.8), channel_id=1, source_target_pairs={{0,4},{4,0},{1,5},{5,1},{2,6},{6,2},{3,7},{7,3},{8,12},{12,8},{9,1... | collective-permute-start | bytes 1179656 | tf_op jit(solution)/shard_map/ppermute | solution.py:38
  3.7 1.5 %collective-permute-start.1 = (bf16[32,1536]{1,0:T(8,128)(2,1)}, bf16[32,1536]{1,0:T(8,128)(2,1)S(1)}, u32[]{:S(2)}, u32[]{:S(2)}) collective-permute-start(bf16[32,1536]{1,0:T(8,128)(2,1)} %bitcast.10), channel_id=1, source_target_pairs={{0,2},{1,3},{2,0},{3,1},{4,6},{5,7},{6,4},{7,5},{8,10},{9,11},{10,... | collective-permute-start | bytes 294920 | tf_op jit(solution)/shard_map/ppermute | solution.py:38
  5.2 3.9 %load.1 = (bf16[1536,3072]{1,0:T(8,128)(2,1)S(1)}, bf16[3072,1024]{1,0:T(8,128)(2,1)S(1)}, bf16[32,1536]{1,0:T(8,128)(2,1)S(1)}, bf16[64,3072]{1,0:T(8,128)(2,1)S(1)}) custom-call(bf16[1536,3072]{1,0:T(8,128)(2,1)} %bitcast.6, bf16[32,1536]{1,0:T(8,128)(2,1)} %bitcast.11, bf16[64,3072]{1,0:T(8,128)(2,1)} %bitcast.9), custom_call_target="tpu_custom_call" | custom-call | bytes 18874368 | tf_op jit(solution)/shard_map/load/pallas_call | solution.py:66
  9.1 0.0 collective-permute-done.1.across
  9.1 0.1 collective-permute-start.2
  9.2 0.0 copy-done
  9.2 0.5 %collective-permute-start = (bf16[32,1536]{1,0:T(8,128)(2,1)S(1)}, bf16[32,1536]{1,0:T(8,128)(2,1)S(1)}, u32[]{:S(2)}, u32[]{:S(2)}) collective-permute-start(bf16[32,1536]{1,0:T(8,128)(2,1)S(1)} %bitcast.12), channel_id=1, source_target_pairs={{0,1},{1,0},{2,3},{3,2},{4,5},{5,4},{6,7},{7,6},{8,9},{9,8},{10,11... | collective-permute-start | bytes 294920 | tf_op jit(solution)/shard_map/ppermute | solution.py:38
  9.7 1.0 %turn.1.second = bf16[3072,512]{1,0:T(8,128)(2,1)S(1)} custom-call(bf16[1536,3072]{1,0:T(8,128)(2,1)S(1)} %get-tuple-element.30.weight), custom_call_target="tpu_custom_call" | custom-call | flops 805306368 | bytes 6291456 | tf_op jit(solution)/shard_map/turn/pallas_call | solution.py:66
  10.7 0.0 collective-permute-done.2.diagonal
  10.7 0.0 collective-permute-done.beside
  10.7 1.4 %forward.1 = (bf16[128,1536]{1,0:T(8,128)(2,1)S(1)}, bf16[64,3072]{1,0:T(8,128)(2,1)S(1)}, bf16[64,3072]{1,0:T(8,128)(2,1)S(1)}) custom-call(bf16[32,1536]{1,0:T(8,128)(2,1)S(1)} %get-tuple-element.27.own, bf16[32,1536]{1,0:T(8,128)(2,1)S(1)} %collective-permute-done.beside, bf16[32,1536]{1,0:T(8,128)(2,1)S(1)} %collective-permute-done.1.across, ...), custom_call_target="tpu_custom_call" | custom-call | flops 1207959552 | bytes 9437184 | tf_op jit(solution)/shard_map/forward/pallas_call | solution.py:66
  12.2 0.6 %collective-permute-start.3 = (bf16[64,3072]{1,0:T(8,128)(2,1)S(1)}, bf16[64,3072]{1,0:T(8,128)(2,1)S(1)}, u32[]{:S(2)}, u32[]{:S(2)}) collective-permute-start(bf16[64,3072]{1,0:T(8,128)(2,1)S(1)} %get-tuple-element.33), channel_id=1, source_target_pairs={{0,4},{4,0},{1,5},{5,1},{2,6},{6,2},{3,7},{7,3},{8,12},{12,8},{9,1... | collective-permute-start | bytes 1179656 | tf_op jit(solution)/shard_map/ppermute | solution.py:38
  12.7 0.3 %collective-permute-done.4.other = bf16[64,3072]{1,0:T(8,128)(2,1)S(1)} collective-permute-done((bf16[64,3072]{1,0:T(8,128)(2,1)}, bf16[64,3072]{1,0:T(8,128)(2,1)S(1)}, u32[]{:S(2)}, u32[]{:S(2)}) %collective-permute-start.4) | collective-permute-done | bytes 393248 | tf_op jit(solution)/shard_map/ppermute | solution.py:38
  13.0 1.4 %input_grad.1 = (bf16[64,1536]{1,0:T(8,128)(2,1)S(1)}, f32[64,1536]{1,0:T(8,128)S(1)}) custom-call(bf16[64,3072]{1,0:T(8,128)(2,1)S(1)} %collective-permute-done.4.other, bf16[64,3072]{1,0:T(8,128)(2,1)S(1)} %get-tuple-element.35.own, bf16[3072,1024]{1,0:T(8,128)(2,1)S(1)} %get-tuple-element.36.first, bf16[3072,512]{1,0:T(8,128)(2,1)S(1)} %turn.1.second), custom_call_target="tpu_custom_call" | custom-call | flops 1207959552 | bytes 9437184 | tf_op jit(solution)/shard_map/input_grad/pallas_call | solution.py:66
  14.4 0.1 collective-permute-start.5
  14.5 1.4 %collective-permute-done.5.received = bf16[64,1536]{1,0:T(8,128)(2,1)S(1)} collective-permute-done((bf16[64,1536]{1,0:T(8,128)(2,1)S(1)}, bf16[64,1536]{1,0:T(8,128)(2,1)S(1)}, u32[]{:S(2)}, u32[]{:S(2)}) %collective-permute-start.5) | collective-permute-done | bytes 196640 | tf_op jit(solution)/shard_map/ppermute | solution.py:38
  15.9 2.8 %collective-permute-start.6 = (bf16[32,1536]{1,0:T(8,128)(2,1)S(1)}, bf16[32,1536]{1,0:T(8,128)(2,1)S(1)}, u32[]{:S(2)}, u32[]{:S(2)}) collective-permute-start(bf16[32,1536]{1,0:T(8,128)(2,1)S(1)} %get-tuple-element.44), channel_id=1, source_target_pairs={{0,10},{1,11},{2,8},{3,9},{8,2},{9,3},{10,0},{11,1},{16,26},{17,27... | collective-permute-start | bytes 294920 | tf_op jit(solution)/shard_map/ppermute | solution.py:33
  18.7 0.4 %collective-permute-start.7 = (bf16[32,1536]{1,0:T(8,128)(2,1)S(1)}, bf16[32,1536]{1,0:T(8,128)(2,1)S(1)}, u32[]{:S(2)}, u32[]{:S(2)}) collective-permute-start(bf16[32,1536]{1,0:T(8,128)(2,1)S(1)} %get-tuple-element.45), channel_id=1, source_target_pairs={{0,8},{1,9},{2,10},{3,11},{8,0},{9,1},{10,2},{11,3},{16,24},{17,25... | collective-permute-start | bytes 294920 | tf_op jit(solution)/shard_map/ppermute | solution.py:33
  19.2 0.0 collective-permute-start.8
  19.2 0.5 %collective-permute-start.9 = (bf16[32,1536]{1,0:T(8,128)(2,1)S(1)}, bf16[32,1536]{1,0:T(8,128)(2,1)S(1)}, u32[]{:S(2)}, u32[]{:S(2)}) collective-permute-start(bf16[32,1536]{1,0:T(8,128)(2,1)S(1)} %get-tuple-element.47), channel_id=1, source_target_pairs={{0,1},{1,0},{2,3},{3,2},{8,16},{9,17},{10,18},{11,19},{16,8},{17,9... | collective-permute-start | bytes 294920 | tf_op jit(solution)/shard_map/ppermute | solution.py:33
  19.7 4.3 %weight_grad.1 = bf16[1536,3072]{1,0:T(8,128)(2,1)} custom-call(bf16[128,1536]{1,0:T(8,128)(2,1)S(1)} %get-tuple-element.49.tokens, bf16[64,3072]{1,0:T(8,128)(2,1)S(1)} %collective-permute-done.4.other, bf16[64,3072]{1,0:T(8,128)(2,1)S(1)} %get-tuple-element.35.own), custom_call_target="tpu_custom_call" | custom-call | flops 1207959552 | bytes 9437184 | tf_op jit(solution)/shard_map/weight_grad/pallas_call | solution.py:66
  24.0 0.0 collective-permute-done.3.hidden_received
  24.0 0.0 collective-permute-done.6.refs_0_
  24.0 0.1 collective-permute-done.7.refs_1_
  24.1 0.0 collective-permute-done.8.refs_2_
  24.1 0.0 collective-permute-done.9.refs_3_
  24.1 0.8 %final_sum.1 = (bf16[64,3072]{1,0:T(8,128)(2,1)}, bf16[32,1536]{1,0:T(8,128)(2,1)}) custom-call(bf16[64,3072]{1,0:T(8,128)(2,1)S(1)} %get-tuple-element.32.hidden_keep, bf16[64,3072]{1,0:T(8,128)(2,1)S(1)} %collective-permute-done.3.hidden_received, bf16[32,1536]{1,0:T(8,128)(2,1)S(1)} %collective-permute-done.6.refs_0_, ...), custom_call_target="tpu_custom_call" | custom-call | bytes 1572864 | tf_op jit(solution)/shard_map/final_sum/pallas_call | solution.py:66
  (1 shorter events, 0.0 us)
Async XLA Ops:
  0.6 8.6 %copy-start = (bf16[1,32,1536]{2,1,0:T(8,128)(2,1)S(1)}, bf16[1,32,1536]{2,1,0:T(8,128)(2,1)}, u32[]{:S(2)}) copy-start(bf16[1,32,1536]{2,1,0:T(8,128)(2,1)} %param.3) | copy-start | bytes 294916
  0.6 12.4 %collective-permute-start.4 = (bf16[64,3072]{1,0:T(8,128)(2,1)}, bf16[64,3072]{1,0:T(8,128)(2,1)S(1)}, u32[]{:S(2)}, u32[]{:S(2)}) collective-permute-start(bf16[64,3072]{1,0:T(8,128)(2,1)} %bitcast.8), channel_id=1, source_target_pairs={{0,4},{4,0},{1,5},{5,1},{2,6},{6,2},{3,7},{7,3},{8,12},{12,8},{9,1... | collective-permute-start | bytes 1179656 | tf_op jit(solution)/shard_map/ppermute | solution.py:38
  3.7 5.4 %collective-permute-start.1 = (bf16[32,1536]{1,0:T(8,128)(2,1)}, bf16[32,1536]{1,0:T(8,128)(2,1)S(1)}, u32[]{:S(2)}, u32[]{:S(2)}) collective-permute-start(bf16[32,1536]{1,0:T(8,128)(2,1)} %bitcast.10), channel_id=1, source_target_pairs={{0,2},{1,3},{2,0},{3,1},{4,6},{5,7},{6,4},{7,5},{8,10},{9,11},{10,... | collective-permute-start | bytes 294920 | tf_op jit(solution)/shard_map/ppermute | solution.py:38
  9.1 1.6 %collective-permute-start.2 = (bf16[32,1536]{1,0:T(8,128)(2,1)S(1)}, bf16[32,1536]{1,0:T(8,128)(2,1)S(1)}, u32[]{:S(2)}, u32[]{:S(2)}) collective-permute-start(bf16[32,1536]{1,0:T(8,128)(2,1)S(1)} %collective-permute-done.1.across), channel_id=1, source_target_pairs={{0,1},{1,0},{2,3},{3,2},{4,5},{5,4},{6,7},{7,6},{8,9},{9,8},{10,11... | collective-permute-start | bytes 294920 | tf_op jit(solution)/shard_map/ppermute | solution.py:38
  9.2 1.5 %collective-permute-start = (bf16[32,1536]{1,0:T(8,128)(2,1)S(1)}, bf16[32,1536]{1,0:T(8,128)(2,1)S(1)}, u32[]{:S(2)}, u32[]{:S(2)}) collective-permute-start(bf16[32,1536]{1,0:T(8,128)(2,1)S(1)} %bitcast.12), channel_id=1, source_target_pairs={{0,1},{1,0},{2,3},{3,2},{4,5},{5,4},{6,7},{7,6},{8,9},{9,8},{10,11... | collective-permute-start | bytes 294920 | tf_op jit(solution)/shard_map/ppermute | solution.py:38
  12.2 11.9 %collective-permute-start.3 = (bf16[64,3072]{1,0:T(8,128)(2,1)S(1)}, bf16[64,3072]{1,0:T(8,128)(2,1)S(1)}, u32[]{:S(2)}, u32[]{:S(2)}) collective-permute-start(bf16[64,3072]{1,0:T(8,128)(2,1)S(1)} %get-tuple-element.33), channel_id=1, source_target_pairs={{0,4},{4,0},{1,5},{5,1},{2,6},{6,2},{3,7},{7,3},{8,12},{12,8},{9,1... | collective-permute-start | bytes 1179656 | tf_op jit(solution)/shard_map/ppermute | solution.py:38
  14.4 1.5 %collective-permute-start.5 = (bf16[64,1536]{1,0:T(8,128)(2,1)S(1)}, bf16[64,1536]{1,0:T(8,128)(2,1)S(1)}, u32[]{:S(2)}, u32[]{:S(2)}) collective-permute-start(bf16[64,1536]{1,0:T(8,128)(2,1)S(1)} %get-tuple-element.39), channel_id=1, source_target_pairs={{0,1},{1,0},{2,3},{3,2},{4,5},{5,4},{6,7},{7,6},{8,9},{9,8},{10,11... | collective-permute-start | bytes 589832 | tf_op jit(solution)/shard_map/ppermute | solution.py:38
  15.9 8.1 %collective-permute-start.6 = (bf16[32,1536]{1,0:T(8,128)(2,1)S(1)}, bf16[32,1536]{1,0:T(8,128)(2,1)S(1)}, u32[]{:S(2)}, u32[]{:S(2)}) collective-permute-start(bf16[32,1536]{1,0:T(8,128)(2,1)S(1)} %get-tuple-element.44), channel_id=1, source_target_pairs={{0,10},{1,11},{2,8},{3,9},{8,2},{9,3},{10,0},{11,1},{16,26},{17,27... | collective-permute-start | bytes 294920 | tf_op jit(solution)/shard_map/ppermute | solution.py:33
  18.7 5.4 %collective-permute-start.7 = (bf16[32,1536]{1,0:T(8,128)(2,1)S(1)}, bf16[32,1536]{1,0:T(8,128)(2,1)S(1)}, u32[]{:S(2)}, u32[]{:S(2)}) collective-permute-start(bf16[32,1536]{1,0:T(8,128)(2,1)S(1)} %get-tuple-element.45), channel_id=1, source_target_pairs={{0,8},{1,9},{2,10},{3,11},{8,0},{9,1},{10,2},{11,3},{16,24},{17,25... | collective-permute-start | bytes 294920 | tf_op jit(solution)/shard_map/ppermute | solution.py:33
  19.2 4.9 %collective-permute-start.8 = (bf16[32,1536]{1,0:T(8,128)(2,1)S(1)}, bf16[32,1536]{1,0:T(8,128)(2,1)S(1)}, u32[]{:S(2)}, u32[]{:S(2)}) collective-permute-start(bf16[32,1536]{1,0:T(8,128)(2,1)S(1)} %get-tuple-element.46), channel_id=1, source_target_pairs={{0,1},{1,0},{2,3},{3,2},{8,18},{9,19},{10,16},{11,17},{16,10},{17,... | collective-permute-start | bytes 294920 | tf_op jit(solution)/shard_map/ppermute | solution.py:33
  19.2 4.9 %collective-permute-start.9 = (bf16[32,1536]{1,0:T(8,128)(2,1)S(1)}, bf16[32,1536]{1,0:T(8,128)(2,1)S(1)}, u32[]{:S(2)}, u32[]{:S(2)}) collective-permute-start(bf16[32,1536]{1,0:T(8,128)(2,1)S(1)} %get-tuple-element.47), channel_id=1, source_target_pairs={{0,1},{1,0},{2,3},{3,2},{8,16},{9,17},{10,18},{11,19},{16,8},{17,9... | collective-permute-start | bytes 294920 | tf_op jit(solution)/shard_map/ppermute | solution.py:33

commit v6 on v5

--- a/solution.py
+++ b/solution.py
@@ -194,19 +194,14 @@
         copy.wait()
 
 
-def sum_kernel(hidden_keep, hidden_received, *refs):
-    *received, hidden_out, passed_out, hidden_held, passed_held, sems = refs
-    copies = []
-    rows = hidden_keep.shape[0] // 2
-    for index in range(2):
-        part = pl.ds(index * rows, rows)
-        hidden_held[part, :] = (
-            hidden_keep[part, :].astype(F32) + hidden_received[part, :].astype(F32)
-        ).astype(BF16)
-        copies.append(
-            pltpu.make_async_copy(hidden_held.at[part], hidden_out.at[part], sems.at[index])
-        )
-        copies[-1].start()
+def hidden_kernel(keep, received, out):
+    out[...] = (keep[...].astype(F32) + received[...].astype(F32)).astype(BF16)
+
+
+def sum_kernel(hidden, *refs):
+    *received, hidden_out, passed_out, passed_held, sems = refs
+    copies = [pltpu.make_async_copy(hidden, hidden_out, sems.at[0])]
+    copies[0].start()
     sums = [
         received[index][...].astype(F32) + received[index + 1][...].astype(F32)
         for index in (0, 2)
@@ -215,7 +210,7 @@
     last = section == lax.axis_size("section") - 1
     passed = jnp.where(section % 2 == 0, sums[0], sums[1])
     passed_held[...] = jnp.where(last, jnp.zeros_like(passed), passed).astype(BF16)
-    copies.append(pltpu.make_async_copy(passed_held, passed_out, sems.at[2]))
+    copies.append(pltpu.make_async_copy(passed_held, passed_out, sems.at[1]))
     copies[-1].start()
     for copy in copies:
         copy.wait()
@@ -307,14 +302,21 @@
         moved=2 * width * units,
         name="weight_grad",
     )
+    hidden_received, weight_grad = lax.optimization_barrier((hidden_received, weight_grad))
+    hidden = call(
+        hidden_kernel,
+        jax.ShapeDtypeStruct((half, units), BF16),
+        (hidden_keep, hidden_received),
+        moved=6 * half * units,
+        name="hidden_sum",
+    )
     hidden, passed_grad = call(
         sum_kernel,
         [jax.ShapeDtypeStruct((half, units), BF16), jax.ShapeDtypeStruct((rows, width), BF16)],
-        [hidden_keep, hidden_received] + received,
+        [hidden] + received,
         scratch=[
-            pltpu.VMEM((half, units), BF16),
             pltpu.VMEM((rows, width), BF16),
-            pltpu.SemaphoreType.DMA((3,)),
+            pltpu.SemaphoreType.DMA((2,)),
         ],
         out_specs=[anywhere] * 2,
         moved=8 * half * units,

time: 25.3 us -> 25.3 us (level)
    pallas_call x7 -> x8, Pallas kernels: 13 us -> 13 us  [call(): pl.pallas_call(kernel, grid=grid, out_shape=shapes, in_specs=in_specs, ou...]
  transfers between devices with their start and end apart: 10 -> 10, of which waited for: 3 -> 2; matrix products, arithmetic and copies ran while one was open for 0% -> 0% of each run, Pallas kernels for 48% -> 49%
where the time goes in v6:
time: 25.3 us; the launch traced here: 25 us
  Pallas kernels  13 us (51%)
  starting transfers between devices  9.48 us (37%)
  waiting for transfers between devices  1.72 us (7%)
  between operations  0.78 us (3%)
    pallas_call x8, Pallas kernels, call(): pl.pallas_call(kernel, grid=grid, out_shape=shapes, in_specs=in_specs, ou...  13 us
    ppermute x6, starting transfers between devices, swapped(): lax.ppermute(value, axis, [(source, source ^ distance) for source in rang...  5.73 us
    ppermute x4, starting transfers between devices, paired_sections(): return lax.ppermute(value, ('section', 'col'), pairs)  3.75 us
    ppermute x6, waiting for transfers between devices, swapped(): lax.ppermute(value, axis, [(source, source ^ distance) for source in rang...  1.71 us
  transfers between devices with their start and end apart: 10, of which 2 were waited for; matrix products, arithmetic and copies ran while one was open for 0% of the time, Pallas kernels for 49%

profile of v6, /device:TPU:0, one launch (start us, length us, event | category | flops | bytes accessed | tf_op | source)
XLA Modules:
  0.0 25.0 jit_solution(3443968377635262593)
XLA Ops:
  0.6 0.0 copy-start
  0.6 3.0 %collective-permute-start.4 = (bf16[64,3072]{1,0:T(8,128)(2,1)}, bf16[64,3072]{1,0:T(8,128)(2,1)S(1)}, u32[]{:S(2)}, u32[]{:S(2)}) collective-permute-start(bf16[64,3072]{1,0:T(8,128)(2,1)} %bitcast.8), channel_id=1, source_target_pairs={{0,4},{4,0},{1,5},{5,1},{2,6},{6,2},{3,7},{7,3},{8,12},{12,8},{9,1... | collective-permute-start | bytes 1179656 | tf_op jit(solution)/shard_map/ppermute | solution.py:38
  3.7 1.5 %collective-permute-start.1 = (bf16[32,1536]{1,0:T(8,128)(2,1)}, bf16[32,1536]{1,0:T(8,128)(2,1)S(1)}, u32[]{:S(2)}, u32[]{:S(2)}) collective-permute-start(bf16[32,1536]{1,0:T(8,128)(2,1)} %bitcast.10), channel_id=1, source_target_pairs={{0,2},{1,3},{2,0},{3,1},{4,6},{5,7},{6,4},{7,5},{8,10},{9,11},{10,... | collective-permute-start | bytes 294920 | tf_op jit(solution)/shard_map/ppermute | solution.py:38
  5.2 3.9 %load.1 = (bf16[1536,3072]{1,0:T(8,128)(2,1)S(1)}, bf16[3072,1024]{1,0:T(8,128)(2,1)S(1)}, bf16[32,1536]{1,0:T(8,128)(2,1)S(1)}, bf16[64,3072]{1,0:T(8,128)(2,1)S(1)}) custom-call(bf16[1536,3072]{1,0:T(8,128)(2,1)} %bitcast.6, bf16[32,1536]{1,0:T(8,128)(2,1)} %bitcast.11, bf16[64,3072]{1,0:T(8,128)(2,1)} %bitcast.9), custom_call_target="tpu_custom_call" | custom-call | bytes 18874368 | tf_op jit(solution)/shard_map/load/pallas_call | solution.py:66
  9.1 0.0 collective-permute-done.1.across
  9.1 0.1 collective-permute-start.2
  9.2 0.0 copy-done
  9.2 0.5 %collective-permute-start = (bf16[32,1536]{1,0:T(8,128)(2,1)S(1)}, bf16[32,1536]{1,0:T(8,128)(2,1)S(1)}, u32[]{:S(2)}, u32[]{:S(2)}) collective-permute-start(bf16[32,1536]{1,0:T(8,128)(2,1)S(1)} %bitcast.12), channel_id=1, source_target_pairs={{0,1},{1,0},{2,3},{3,2},{4,5},{5,4},{6,7},{7,6},{8,9},{9,8},{10,11... | collective-permute-start | bytes 294920 | tf_op jit(solution)/shard_map/ppermute | solution.py:38
  9.7 1.0 %turn.1.second = bf16[3072,512]{1,0:T(8,128)(2,1)S(1)} custom-call(bf16[1536,3072]{1,0:T(8,128)(2,1)S(1)} %get-tuple-element.32.weight), custom_call_target="tpu_custom_call" | custom-call | flops 805306368 | bytes 6291456 | tf_op jit(solution)/shard_map/turn/pallas_call | solution.py:66
  10.7 0.0 collective-permute-done.2.diagonal
  10.7 0.0 collective-permute-done.beside
  10.7 1.4 %forward.1 = (bf16[128,1536]{1,0:T(8,128)(2,1)S(1)}, bf16[64,3072]{1,0:T(8,128)(2,1)S(1)}, bf16[64,3072]{1,0:T(8,128)(2,1)S(1)}) custom-call(bf16[32,1536]{1,0:T(8,128)(2,1)S(1)} %get-tuple-element.29.own, bf16[32,1536]{1,0:T(8,128)(2,1)S(1)} %collective-permute-done.beside, bf16[32,1536]{1,0:T(8,128)(2,1)S(1)} %collective-permute-done.1.across, ...), custom_call_target="tpu_custom_call" | custom-call | flops 1207959552 | bytes 9437184 | tf_op jit(solution)/shard_map/forward/pallas_call | solution.py:66
  12.2 0.6 %collective-permute-start.3 = (bf16[64,3072]{1,0:T(8,128)(2,1)S(1)}, bf16[64,3072]{1,0:T(8,128)(2,1)S(1)}, u32[]{:S(2)}, u32[]{:S(2)}) collective-permute-start(bf16[64,3072]{1,0:T(8,128)(2,1)S(1)} %get-tuple-element.35), channel_id=1, source_target_pairs={{0,4},{4,0},{1,5},{5,1},{2,6},{6,2},{3,7},{7,3},{8,12},{12,8},{9,1... | collective-permute-start | bytes 1179656 | tf_op jit(solution)/shard_map/ppermute | solution.py:38
  12.7 0.3 %collective-permute-done.4.other = bf16[64,3072]{1,0:T(8,128)(2,1)S(1)} collective-permute-done((bf16[64,3072]{1,0:T(8,128)(2,1)}, bf16[64,3072]{1,0:T(8,128)(2,1)S(1)}, u32[]{:S(2)}, u32[]{:S(2)}) %collective-permute-start.4) | collective-permute-done | bytes 393248 | tf_op jit(solution)/shard_map/ppermute | solution.py:38
  13.0 1.4 %input_grad.1 = (bf16[64,1536]{1,0:T(8,128)(2,1)S(1)}, f32[64,1536]{1,0:T(8,128)S(1)}) custom-call(bf16[64,3072]{1,0:T(8,128)(2,1)S(1)} %collective-permute-done.4.other, bf16[64,3072]{1,0:T(8,128)(2,1)S(1)} %get-tuple-element.37.own, bf16[3072,1024]{1,0:T(8,128)(2,1)S(1)} %get-tuple-element.38.first, bf16[3072,512]{1,0:T(8,128)(2,1)S(1)} %turn.1.second), custom_call_target="tpu_custom_call" | custom-call | flops 1207959552 | bytes 9437184 | tf_op jit(solution)/shard_map/input_grad/pallas_call | solution.py:66
  14.4 0.1 collective-permute-start.5
  14.5 1.4 %collective-permute-done.5.received = bf16[64,1536]{1,0:T(8,128)(2,1)S(1)} collective-permute-done((bf16[64,1536]{1,0:T(8,128)(2,1)S(1)}, bf16[64,1536]{1,0:T(8,128)(2,1)S(1)}, u32[]{:S(2)}, u32[]{:S(2)}) %collective-permute-start.5) | collective-permute-done | bytes 196640 | tf_op jit(solution)/shard_map/ppermute | solution.py:38
  15.9 2.8 %collective-permute-start.6 = (bf16[32,1536]{1,0:T(8,128)(2,1)S(1)}, bf16[32,1536]{1,0:T(8,128)(2,1)S(1)}, u32[]{:S(2)}, u32[]{:S(2)}) collective-permute-start(bf16[32,1536]{1,0:T(8,128)(2,1)S(1)} %get-tuple-element.48), channel_id=1, source_target_pairs={{0,10},{1,11},{2,8},{3,9},{8,2},{9,3},{10,0},{11,1},{16,26},{17,27... | collective-permute-start | bytes 294920 | tf_op jit(solution)/shard_map/ppermute | solution.py:33
  18.7 0.4 %collective-permute-start.7 = (bf16[32,1536]{1,0:T(8,128)(2,1)S(1)}, bf16[32,1536]{1,0:T(8,128)(2,1)S(1)}, u32[]{:S(2)}, u32[]{:S(2)}) collective-permute-start(bf16[32,1536]{1,0:T(8,128)(2,1)S(1)} %get-tuple-element.49), channel_id=1, source_target_pairs={{0,8},{1,9},{2,10},{3,11},{8,0},{9,1},{10,2},{11,3},{16,24},{17,25... | collective-permute-start | bytes 294920 | tf_op jit(solution)/shard_map/ppermute | solution.py:33
  19.2 0.0 collective-permute-start.8
  19.2 0.5 %collective-permute-start.9 = (bf16[32,1536]{1,0:T(8,128)(2,1)S(1)}, bf16[32,1536]{1,0:T(8,128)(2,1)S(1)}, u32[]{:S(2)}, u32[]{:S(2)}) collective-permute-start(bf16[32,1536]{1,0:T(8,128)(2,1)S(1)} %get-tuple-element.51), channel_id=1, source_target_pairs={{0,1},{1,0},{2,3},{3,2},{8,16},{9,17},{10,18},{11,19},{16,8},{17,9... | collective-permute-start | bytes 294920 | tf_op jit(solution)/shard_map/ppermute | solution.py:33
  19.7 4.3 %weight_grad.1 = bf16[1536,3072]{1,0:T(8,128)(2,1)} custom-call(bf16[128,1536]{1,0:T(8,128)(2,1)S(1)} %get-tuple-element.46.tokens, bf16[64,3072]{1,0:T(8,128)(2,1)S(1)} %collective-permute-done.4.other, bf16[64,3072]{1,0:T(8,128)(2,1)S(1)} %get-tuple-element.37.own), custom_call_target="tpu_custom_call" | custom-call | flops 1207959552 | bytes 9437184 | tf_op jit(solution)/shard_map/weight_grad/pallas_call | solution.py:66
  24.0 0.0 collective-permute-done.3.received
  24.0 0.1 hidden_sum.1.hidden
  24.1 0.0 collective-permute-done.6.refs_0_
  24.1 0.0 collective-permute-done.7.refs_1_
  24.2 0.0 collective-permute-done.8.refs_2_
  24.2 0.0 collective-permute-done.9.refs_3_
  24.2 0.8 %final_sum.1 = (bf16[64,3072]{1,0:T(8,128)(2,1)}, bf16[32,1536]{1,0:T(8,128)(2,1)}) custom-call(bf16[64,3072]{1,0:T(8,128)(2,1)S(1)} %hidden_sum.1.hidden, bf16[32,1536]{1,0:T(8,128)(2,1)S(1)} %collective-permute-done.6.refs_0_, bf16[32,1536]{1,0:T(8,128)(2,1)S(1)} %collective-permute-done.7.refs_1_, bf16[32,1536]{1,0:T(8,128)(2,1)S(1)} %collective-permute-done.8.refs_2_, ...), custom_call_target="tpu_custom_call" | custom-call | bytes 1572864 | tf_op jit(solution)/shard_map/final_sum/pallas_call | solution.py:66
  (1 shorter events, 0.0 us)
Async XLA Ops:
  0.6 8.6 %copy-start = (bf16[1,32,1536]{2,1,0:T(8,128)(2,1)S(1)}, bf16[1,32,1536]{2,1,0:T(8,128)(2,1)}, u32[]{:S(2)}) copy-start(bf16[1,32,1536]{2,1,0:T(8,128)(2,1)} %param.3) | copy-start | bytes 294916
  0.6 12.4 %collective-permute-start.4 = (bf16[64,3072]{1,0:T(8,128)(2,1)}, bf16[64,3072]{1,0:T(8,128)(2,1)S(1)}, u32[]{:S(2)}, u32[]{:S(2)}) collective-permute-start(bf16[64,3072]{1,0:T(8,128)(2,1)} %bitcast.8), channel_id=1, source_target_pairs={{0,4},{4,0},{1,5},{5,1},{2,6},{6,2},{3,7},{7,3},{8,12},{12,8},{9,1... | collective-permute-start | bytes 1179656 | tf_op jit(solution)/shard_map/ppermute | solution.py:38
  3.7 5.4 %collective-permute-start.1 = (bf16[32,1536]{1,0:T(8,128)(2,1)}, bf16[32,1536]{1,0:T(8,128)(2,1)S(1)}, u32[]{:S(2)}, u32[]{:S(2)}) collective-permute-start(bf16[32,1536]{1,0:T(8,128)(2,1)} %bitcast.10), channel_id=1, source_target_pairs={{0,2},{1,3},{2,0},{3,1},{4,6},{5,7},{6,4},{7,5},{8,10},{9,11},{10,... | collective-permute-start | bytes 294920 | tf_op jit(solution)/shard_map/ppermute | solution.py:38
  9.1 1.6 %collective-permute-start.2 = (bf16[32,1536]{1,0:T(8,128)(2,1)S(1)}, bf16[32,1536]{1,0:T(8,128)(2,1)S(1)}, u32[]{:S(2)}, u32[]{:S(2)}) collective-permute-start(bf16[32,1536]{1,0:T(8,128)(2,1)S(1)} %collective-permute-done.1.across), channel_id=1, source_target_pairs={{0,1},{1,0},{2,3},{3,2},{4,5},{5,4},{6,7},{7,6},{8,9},{9,8},{10,11... | collective-permute-start | bytes 294920 | tf_op jit(solution)/shard_map/ppermute | solution.py:38
  9.2 1.5 %collective-permute-start = (bf16[32,1536]{1,0:T(8,128)(2,1)S(1)}, bf16[32,1536]{1,0:T(8,128)(2,1)S(1)}, u32[]{:S(2)}, u32[]{:S(2)}) collective-permute-start(bf16[32,1536]{1,0:T(8,128)(2,1)S(1)} %bitcast.12), channel_id=1, source_target_pairs={{0,1},{1,0},{2,3},{3,2},{4,5},{5,4},{6,7},{7,6},{8,9},{9,8},{10,11... | collective-permute-start | bytes 294920 | tf_op jit(solution)/shard_map/ppermute | solution.py:38
  12.2 11.9 %collective-permute-start.3 = (bf16[64,3072]{1,0:T(8,128)(2,1)S(1)}, bf16[64,3072]{1,0:T(8,128)(2,1)S(1)}, u32[]{:S(2)}, u32[]{:S(2)}) collective-permute-start(bf16[64,3072]{1,0:T(8,128)(2,1)S(1)} %get-tuple-element.35), channel_id=1, source_target_pairs={{0,4},{4,0},{1,5},{5,1},{2,6},{6,2},{3,7},{7,3},{8,12},{12,8},{9,1... | collective-permute-start | bytes 1179656 | tf_op jit(solution)/shard_map/ppermute | solution.py:38
  14.4 1.5 %collective-permute-start.5 = (bf16[64,1536]{1,0:T(8,128)(2,1)S(1)}, bf16[64,1536]{1,0:T(8,128)(2,1)S(1)}, u32[]{:S(2)}, u32[]{:S(2)}) collective-permute-start(bf16[64,1536]{1,0:T(8,128)(2,1)S(1)} %get-tuple-element.41), channel_id=1, source_target_pairs={{0,1},{1,0},{2,3},{3,2},{4,5},{5,4},{6,7},{7,6},{8,9},{9,8},{10,11... | collective-permute-start | bytes 589832 | tf_op jit(solution)/shard_map/ppermute | solution.py:38
  15.9 8.2 %collective-permute-start.6 = (bf16[32,1536]{1,0:T(8,128)(2,1)S(1)}, bf16[32,1536]{1,0:T(8,128)(2,1)S(1)}, u32[]{:S(2)}, u32[]{:S(2)}) collective-permute-start(bf16[32,1536]{1,0:T(8,128)(2,1)S(1)} %get-tuple-element.48), channel_id=1, source_target_pairs={{0,10},{1,11},{2,8},{3,9},{8,2},{9,3},{10,0},{11,1},{16,26},{17,27... | collective-permute-start | bytes 294920 | tf_op jit(solution)/shard_map/ppermute | solution.py:33
  18.7 5.4 %collective-permute-start.7 = (bf16[32,1536]{1,0:T(8,128)(2,1)S(1)}, bf16[32,1536]{1,0:T(8,128)(2,1)S(1)}, u32[]{:S(2)}, u32[]{:S(2)}) collective-permute-start(bf16[32,1536]{1,0:T(8,128)(2,1)S(1)} %get-tuple-element.49), channel_id=1, source_target_pairs={{0,8},{1,9},{2,10},{3,11},{8,0},{9,1},{10,2},{11,3},{16,24},{17,25... | collective-permute-start | bytes 294920 | tf_op jit(solution)/shard_map/ppermute | solution.py:33
  19.2 5.0 %collective-permute-start.8 = (bf16[32,1536]{1,0:T(8,128)(2,1)S(1)}, bf16[32,1536]{1,0:T(8,128)(2,1)S(1)}, u32[]{:S(2)}, u32[]{:S(2)}) collective-permute-start(bf16[32,1536]{1,0:T(8,128)(2,1)S(1)} %get-tuple-element.50), channel_id=1, source_target_pairs={{0,1},{1,0},{2,3},{3,2},{8,18},{9,19},{10,16},{11,17},{16,10},{17,... | collective-permute-start | bytes 294920 | tf_op jit(solution)/shard_map/ppermute | solution.py:33
  19.2 5.0 %collective-permute-start.9 = (bf16[32,1536]{1,0:T(8,128)(2,1)S(1)}, bf16[32,1536]{1,0:T(8,128)(2,1)S(1)}, u32[]{:S(2)}, u32[]{:S(2)}) collective-permute-start(bf16[32,1536]{1,0:T(8,128)(2,1)S(1)} %get-tuple-element.51), channel_id=1, source_target_pairs={{0,1},{1,0},{2,3},{3,2},{8,16},{9,17},{10,18},{11,19},{16,8},{17,9... | collective-permute-start | bytes 294920 | tf_op jit(solution)/shard_map/ppermute | solution.py:33

commit v7 on v6

--- a/solution.py
+++ b/solution.py
@@ -180,9 +180,12 @@
         grads = jnp.concatenate(
             [other[:, lower : lower + tile], own[:, lower : lower + tile]], axis=0
         )
-        blocks[index] = jnp.dot(turned[...], grads, preferred_element_type=F32).astype(BF16)
         rows = out.shape[0] // 2
         for part in range(2):
+            tall = pl.ds(part * rows, rows)
+            blocks[index, tall, :] = jnp.dot(
+                turned[tall, :], grads, preferred_element_type=F32
+            ).astype(BF16)
             copy = pltpu.make_async_copy(
                 blocks.at[index, pl.ds(part * rows, rows)],
                 out.at[pl.ds(part * rows, rows), pl.ds(lower, tile)],

time: 25.3 us -> 25.3 us (level)
  transfers between devices with their start and end apart: 10 -> 10, of which waited for: 2 -> 3; matrix products, arithmetic and copies ran while one was open for 0% -> 0% of each run, Pallas kernels for 49% -> 48%
where the time goes in v7:
time: 25.3 us; the launch traced here: 24.9 us
  Pallas kernels  12.8 us (51%)
  starting transfers between devices  9.48 us (37%)
  waiting for transfers between devices  1.87 us (7%)
  between operations  0.75 us (3%)
    pallas_call x8, Pallas kernels, call(): pl.pallas_call(kernel, grid=grid, out_shape=shapes, in_specs=in_specs, ou...  12.8 us
    ppermute x6, starting transfers between devices, swapped(): lax.ppermute(value, axis, [(source, source ^ distance) for source in rang...  5.73 us
    ppermute x4, starting transfers between devices, paired_sections(): return lax.ppermute(value, ('section', 'col'), pairs)  3.75 us
    ppermute x6, waiting for transfers between devices, swapped(): lax.ppermute(value, axis, [(source, source ^ distance) for source in rang...  1.71 us
  transfers between devices with their start and end apart: 10, of which 3 were waited for; matrix products, arithmetic and copies ran while one was open for 0% of the time, Pallas kernels for 48%

profile of v7, /device:TPU:0, one launch (start us, length us, event | category | flops | bytes accessed | tf_op | source)
XLA Modules:
  0.0 24.9 jit_solution(18141485114391266290)
XLA Ops:
  0.6 0.0 copy-start
  0.6 3.0 %collective-permute-start.4 = (bf16[64,3072]{1,0:T(8,128)(2,1)}, bf16[64,3072]{1,0:T(8,128)(2,1)S(1)}, u32[]{:S(2)}, u32[]{:S(2)}) collective-permute-start(bf16[64,3072]{1,0:T(8,128)(2,1)} %bitcast.8), channel_id=1, source_target_pairs={{0,4},{4,0},{1,5},{5,1},{2,6},{6,2},{3,7},{7,3},{8,12},{12,8},{9,1... | collective-permute-start | bytes 1179656 | tf_op jit(solution)/shard_map/ppermute | solution.py:38
  3.7 1.5 %collective-permute-start.1 = (bf16[32,1536]{1,0:T(8,128)(2,1)}, bf16[32,1536]{1,0:T(8,128)(2,1)S(1)}, u32[]{:S(2)}, u32[]{:S(2)}) collective-permute-start(bf16[32,1536]{1,0:T(8,128)(2,1)} %bitcast.10), channel_id=1, source_target_pairs={{0,2},{1,3},{2,0},{3,1},{4,6},{5,7},{6,4},{7,5},{8,10},{9,11},{10,... | collective-permute-start | bytes 294920 | tf_op jit(solution)/shard_map/ppermute | solution.py:38
  5.2 3.9 %load.1 = (bf16[1536,3072]{1,0:T(8,128)(2,1)S(1)}, bf16[3072,1024]{1,0:T(8,128)(2,1)S(1)}, bf16[32,1536]{1,0:T(8,128)(2,1)S(1)}, bf16[64,3072]{1,0:T(8,128)(2,1)S(1)}) custom-call(bf16[1536,3072]{1,0:T(8,128)(2,1)} %bitcast.6, bf16[32,1536]{1,0:T(8,128)(2,1)} %bitcast.11, bf16[64,3072]{1,0:T(8,128)(2,1)} %bitcast.9), custom_call_target="tpu_custom_call" | custom-call | bytes 18874368 | tf_op jit(solution)/shard_map/load/pallas_call | solution.py:66
  9.1 0.0 collective-permute-done.1.across
  9.1 0.1 collective-permute-start.2
  9.2 0.0 copy-done
  9.2 0.5 %collective-permute-start = (bf16[32,1536]{1,0:T(8,128)(2,1)S(1)}, bf16[32,1536]{1,0:T(8,128)(2,1)S(1)}, u32[]{:S(2)}, u32[]{:S(2)}) collective-permute-start(bf16[32,1536]{1,0:T(8,128)(2,1)S(1)} %bitcast.12), channel_id=1, source_target_pairs={{0,1},{1,0},{2,3},{3,2},{4,5},{5,4},{6,7},{7,6},{8,9},{9,8},{10,11... | collective-permute-start | bytes 294920 | tf_op jit(solution)/shard_map/ppermute | solution.py:38
  9.7 1.0 %turn.1.second = bf16[3072,512]{1,0:T(8,128)(2,1)S(1)} custom-call(bf16[1536,3072]{1,0:T(8,128)(2,1)S(1)} %get-tuple-element.32.weight), custom_call_target="tpu_custom_call" | custom-call | flops 805306368 | bytes 6291456 | tf_op jit(solution)/shard_map/turn/pallas_call | solution.py:66
  10.7 0.0 collective-permute-done.2.diagonal
  10.7 0.0 collective-permute-done.beside
  10.7 1.4 %forward.1 = (bf16[128,1536]{1,0:T(8,128)(2,1)S(1)}, bf16[64,3072]{1,0:T(8,128)(2,1)S(1)}, bf16[64,3072]{1,0:T(8,128)(2,1)S(1)}) custom-call(bf16[32,1536]{1,0:T(8,128)(2,1)S(1)} %get-tuple-element.29.own, bf16[32,1536]{1,0:T(8,128)(2,1)S(1)} %collective-permute-done.beside, bf16[32,1536]{1,0:T(8,128)(2,1)S(1)} %collective-permute-done.1.across, ...), custom_call_target="tpu_custom_call" | custom-call | flops 1207959552 | bytes 9437184 | tf_op jit(solution)/shard_map/forward/pallas_call | solution.py:66
  12.2 0.6 %collective-permute-start.3 = (bf16[64,3072]{1,0:T(8,128)(2,1)S(1)}, bf16[64,3072]{1,0:T(8,128)(2,1)S(1)}, u32[]{:S(2)}, u32[]{:S(2)}) collective-permute-start(bf16[64,3072]{1,0:T(8,128)(2,1)S(1)} %get-tuple-element.35), channel_id=1, source_target_pairs={{0,4},{4,0},{1,5},{5,1},{2,6},{6,2},{3,7},{7,3},{8,12},{12,8},{9,1... | collective-permute-start | bytes 1179656 | tf_op jit(solution)/shard_map/ppermute | solution.py:38
  12.7 0.3 %collective-permute-done.4.other = bf16[64,3072]{1,0:T(8,128)(2,1)S(1)} collective-permute-done((bf16[64,3072]{1,0:T(8,128)(2,1)}, bf16[64,3072]{1,0:T(8,128)(2,1)S(1)}, u32[]{:S(2)}, u32[]{:S(2)}) %collective-permute-start.4) | collective-permute-done | bytes 393248 | tf_op jit(solution)/shard_map/ppermute | solution.py:38
  13.0 1.4 %input_grad.1 = (bf16[64,1536]{1,0:T(8,128)(2,1)S(1)}, f32[64,1536]{1,0:T(8,128)S(1)}) custom-call(bf16[64,3072]{1,0:T(8,128)(2,1)S(1)} %collective-permute-done.4.other, bf16[64,3072]{1,0:T(8,128)(2,1)S(1)} %get-tuple-element.37.own, bf16[3072,1024]{1,0:T(8,128)(2,1)S(1)} %get-tuple-element.38.first, bf16[3072,512]{1,0:T(8,128)(2,1)S(1)} %turn.1.second), custom_call_target="tpu_custom_call" | custom-call | flops 1207959552 | bytes 9437184 | tf_op jit(solution)/shard_map/input_grad/pallas_call | solution.py:66
  14.4 0.1 collective-permute-start.5
  14.5 1.4 %collective-permute-done.5.received = bf16[64,1536]{1,0:T(8,128)(2,1)S(1)} collective-permute-done((bf16[64,1536]{1,0:T(8,128)(2,1)S(1)}, bf16[64,1536]{1,0:T(8,128)(2,1)S(1)}, u32[]{:S(2)}, u32[]{:S(2)}) %collective-permute-start.5) | collective-permute-done | bytes 196640 | tf_op jit(solution)/shard_map/ppermute | solution.py:38
  15.9 2.8 %collective-permute-start.6 = (bf16[32,1536]{1,0:T(8,128)(2,1)S(1)}, bf16[32,1536]{1,0:T(8,128)(2,1)S(1)}, u32[]{:S(2)}, u32[]{:S(2)}) collective-permute-start(bf16[32,1536]{1,0:T(8,128)(2,1)S(1)} %get-tuple-element.48), channel_id=1, source_target_pairs={{0,10},{1,11},{2,8},{3,9},{8,2},{9,3},{10,0},{11,1},{16,26},{17,27... | collective-permute-start | bytes 294920 | tf_op jit(solution)/shard_map/ppermute | solution.py:33
  18.7 0.4 %collective-permute-start.7 = (bf16[32,1536]{1,0:T(8,128)(2,1)S(1)}, bf16[32,1536]{1,0:T(8,128)(2,1)S(1)}, u32[]{:S(2)}, u32[]{:S(2)}) collective-permute-start(bf16[32,1536]{1,0:T(8,128)(2,1)S(1)} %get-tuple-element.49), channel_id=1, source_target_pairs={{0,8},{1,9},{2,10},{3,11},{8,0},{9,1},{10,2},{11,3},{16,24},{17,25... | collective-permute-start | bytes 294920 | tf_op jit(solution)/shard_map/ppermute | solution.py:33
  19.2 0.0 collective-permute-start.8
  19.2 0.5 %collective-permute-start.9 = (bf16[32,1536]{1,0:T(8,128)(2,1)S(1)}, bf16[32,1536]{1,0:T(8,128)(2,1)S(1)}, u32[]{:S(2)}, u32[]{:S(2)}) collective-permute-start(bf16[32,1536]{1,0:T(8,128)(2,1)S(1)} %get-tuple-element.51), channel_id=1, source_target_pairs={{0,1},{1,0},{2,3},{3,2},{8,16},{9,17},{10,18},{11,19},{16,8},{17,9... | collective-permute-start | bytes 294920 | tf_op jit(solution)/shard_map/ppermute | solution.py:33
  19.7 4.1 %weight_grad.1 = bf16[1536,3072]{1,0:T(8,128)(2,1)} custom-call(bf16[128,1536]{1,0:T(8,128)(2,1)S(1)} %get-tuple-element.46.tokens, bf16[64,3072]{1,0:T(8,128)(2,1)S(1)} %collective-permute-done.4.other, bf16[64,3072]{1,0:T(8,128)(2,1)S(1)} %get-tuple-element.37.own), custom_call_target="tpu_custom_call" | custom-call | flops 1207959552 | bytes 9437184 | tf_op jit(solution)/shard_map/weight_grad/pallas_call | solution.py:66
  23.8 0.0 collective-permute-done.3.received
  23.8 0.1 hidden_sum.1.hidden
  23.9 0.0 collective-permute-done.6.refs_0_
  23.9 0.2 collective-permute-done.7.refs_1_
  24.1 0.0 collective-permute-done.8.refs_2_
  24.1 0.0 collective-permute-done.9.refs_3_
  24.1 0.8 %final_sum.1 = (bf16[64,3072]{1,0:T(8,128)(2,1)}, bf16[32,1536]{1,0:T(8,128)(2,1)}) custom-call(bf16[64,3072]{1,0:T(8,128)(2,1)S(1)} %hidden_sum.1.hidden, bf16[32,1536]{1,0:T(8,128)(2,1)S(1)} %collective-permute-done.6.refs_0_, bf16[32,1536]{1,0:T(8,128)(2,1)S(1)} %collective-permute-done.7.refs_1_, bf16[32,1536]{1,0:T(8,128)(2,1)S(1)} %collective-permute-done.8.refs_2_, ...), custom_call_target="tpu_custom_call" | custom-call | bytes 1572864 | tf_op jit(solution)/shard_map/final_sum/pallas_call | solution.py:66
  (1 shorter events, 0.0 us)
Async XLA Ops:
  0.6 8.6 %copy-start = (bf16[1,32,1536]{2,1,0:T(8,128)(2,1)S(1)}, bf16[1,32,1536]{2,1,0:T(8,128)(2,1)}, u32[]{:S(2)}) copy-start(bf16[1,32,1536]{2,1,0:T(8,128)(2,1)} %param.3) | copy-start | bytes 294916
  0.6 12.4 %collective-permute-start.4 = (bf16[64,3072]{1,0:T(8,128)(2,1)}, bf16[64,3072]{1,0:T(8,128)(2,1)S(1)}, u32[]{:S(2)}, u32[]{:S(2)}) collective-permute-start(bf16[64,3072]{1,0:T(8,128)(2,1)} %bitcast.8), channel_id=1, source_target_pairs={{0,4},{4,0},{1,5},{5,1},{2,6},{6,2},{3,7},{7,3},{8,12},{12,8},{9,1... | collective-permute-start | bytes 1179656 | tf_op jit(solution)/shard_map/ppermute | solution.py:38
  3.7 5.4 %collective-permute-start.1 = (bf16[32,1536]{1,0:T(8,128)(2,1)}, bf16[32,1536]{1,0:T(8,128)(2,1)S(1)}, u32[]{:S(2)}, u32[]{:S(2)}) collective-permute-start(bf16[32,1536]{1,0:T(8,128)(2,1)} %bitcast.10), channel_id=1, source_target_pairs={{0,2},{1,3},{2,0},{3,1},{4,6},{5,7},{6,4},{7,5},{8,10},{9,11},{10,... | collective-permute-start | bytes 294920 | tf_op jit(solution)/shard_map/ppermute | solution.py:38
  9.1 1.6 %collective-permute-start.2 = (bf16[32,1536]{1,0:T(8,128)(2,1)S(1)}, bf16[32,1536]{1,0:T(8,128)(2,1)S(1)}, u32[]{:S(2)}, u32[]{:S(2)}) collective-permute-start(bf16[32,1536]{1,0:T(8,128)(2,1)S(1)} %collective-permute-done.1.across), channel_id=1, source_target_pairs={{0,1},{1,0},{2,3},{3,2},{4,5},{5,4},{6,7},{7,6},{8,9},{9,8},{10,11... | collective-permute-start | bytes 294920 | tf_op jit(solution)/shard_map/ppermute | solution.py:38
  9.2 1.5 %collective-permute-start = (bf16[32,1536]{1,0:T(8,128)(2,1)S(1)}, bf16[32,1536]{1,0:T(8,128)(2,1)S(1)}, u32[]{:S(2)}, u32[]{:S(2)}) collective-permute-start(bf16[32,1536]{1,0:T(8,128)(2,1)S(1)} %bitcast.12), channel_id=1, source_target_pairs={{0,1},{1,0},{2,3},{3,2},{4,5},{5,4},{6,7},{7,6},{8,9},{9,8},{10,11... | collective-permute-start | bytes 294920 | tf_op jit(solution)/shard_map/ppermute | solution.py:38
  12.2 11.7 %collective-permute-start.3 = (bf16[64,3072]{1,0:T(8,128)(2,1)S(1)}, bf16[64,3072]{1,0:T(8,128)(2,1)S(1)}, u32[]{:S(2)}, u32[]{:S(2)}) collective-permute-start(bf16[64,3072]{1,0:T(8,128)(2,1)S(1)} %get-tuple-element.35), channel_id=1, source_target_pairs={{0,4},{4,0},{1,5},{5,1},{2,6},{6,2},{3,7},{7,3},{8,12},{12,8},{9,1... | collective-permute-start | bytes 1179656 | tf_op jit(solution)/shard_map/ppermute | solution.py:38
  14.4 1.5 %collective-permute-start.5 = (bf16[64,1536]{1,0:T(8,128)(2,1)S(1)}, bf16[64,1536]{1,0:T(8,128)(2,1)S(1)}, u32[]{:S(2)}, u32[]{:S(2)}) collective-permute-start(bf16[64,1536]{1,0:T(8,128)(2,1)S(1)} %get-tuple-element.41), channel_id=1, source_target_pairs={{0,1},{1,0},{2,3},{3,2},{4,5},{5,4},{6,7},{7,6},{8,9},{9,8},{10,11... | collective-permute-start | bytes 589832 | tf_op jit(solution)/shard_map/ppermute | solution.py:38
  15.9 8.0 %collective-permute-start.6 = (bf16[32,1536]{1,0:T(8,128)(2,1)S(1)}, bf16[32,1536]{1,0:T(8,128)(2,1)S(1)}, u32[]{:S(2)}, u32[]{:S(2)}) collective-permute-start(bf16[32,1536]{1,0:T(8,128)(2,1)S(1)} %get-tuple-element.48), channel_id=1, source_target_pairs={{0,10},{1,11},{2,8},{3,9},{8,2},{9,3},{10,0},{11,1},{16,26},{17,27... | collective-permute-start | bytes 294920 | tf_op jit(solution)/shard_map/ppermute | solution.py:33
  18.7 5.4 %collective-permute-start.7 = (bf16[32,1536]{1,0:T(8,128)(2,1)S(1)}, bf16[32,1536]{1,0:T(8,128)(2,1)S(1)}, u32[]{:S(2)}, u32[]{:S(2)}) collective-permute-start(bf16[32,1536]{1,0:T(8,128)(2,1)S(1)} %get-tuple-element.49), channel_id=1, source_target_pairs={{0,8},{1,9},{2,10},{3,11},{8,0},{9,1},{10,2},{11,3},{16,24},{17,25... | collective-permute-start | bytes 294920 | tf_op jit(solution)/shard_map/ppermute | solution.py:33
  19.2 4.9 %collective-permute-start.8 = (bf16[32,1536]{1,0:T(8,128)(2,1)S(1)}, bf16[32,1536]{1,0:T(8,128)(2,1)S(1)}, u32[]{:S(2)}, u32[]{:S(2)}) collective-permute-start(bf16[32,1536]{1,0:T(8,128)(2,1)S(1)} %get-tuple-element.50), channel_id=1, source_target_pairs={{0,1},{1,0},{2,3},{3,2},{8,18},{9,19},{10,16},{11,17},{16,10},{17,... | collective-permute-start | bytes 294920 | tf_op jit(solution)/shard_map/ppermute | solution.py:33
  19.2 4.9 %collective-permute-start.9 = (bf16[32,1536]{1,0:T(8,128)(2,1)S(1)}, bf16[32,1536]{1,0:T(8,128)(2,1)S(1)}, u32[]{:S(2)}, u32[]{:S(2)}) collective-permute-start(bf16[32,1536]{1,0:T(8,128)(2,1)S(1)} %get-tuple-element.51), channel_id=1, source_target_pairs={{0,1},{1,0},{2,3},{3,2},{8,16},{9,17},{10,18},{11,19},{16,8},{17,9... | collective-permute-start | bytes 294920 | tf_op jit(solution)/shard_map/ppermute | solution.py:33

commit v8 on v7

--- a/solution.py
+++ b/solution.py
@@ -164,12 +164,12 @@
     matches = lax.axis_index("col") // 2 == lax.axis_index("row")
     straight = pl.multiple_of(jnp.where(matches, rows, 0), rows)
     crossing = pl.multiple_of(rows - straight, rows)
-    for index, start in enumerate((crossing, straight)):
+    for start, chosen in ((straight, (0, 3)), (crossing, (1, 2))):
         total = (
             keep[pl.ds(start, rows), :] + received[pl.ds(start, rows), :].astype(F32)
         ).astype(BF16)
-        for out in outs[index::2]:
-            out[...] = total
+        for index in chosen:
+            outs[index][...] = total
 
 
 def weight_grad_kernel(tokens, other, own, out, turned, blocks, sems, *, tile):
@@ -288,7 +288,7 @@
     )
     tokens_late, *pieces = lax.optimization_barrier((tokens_all, *pieces))
     received = [
-        paired_sections(piece, index // 2, index % 2 == 0) for index, piece in enumerate(pieces)
+        paired_sections(piece, index // 2, index in (1, 2)) for index, piece in enumerate(pieces)
     ]
     block = 512
     weight_grad = call(

time: 25.3 us -> 25.4 us (level)
  the two profiles are of different devices: /device:TPU:0 before, /device:TPU:16 now
where the time goes in v8:
time: 25.4 us; the launch traced here: 25.3 us
  Pallas kernels  12.8 us (50%)
  starting transfers between devices  9.3 us (37%)
  waiting for transfers between devices  2.42 us (10%)
  between operations  0.76 us (3%)
    pallas_call x8, Pallas kernels, call(): pl.pallas_call(kernel, grid=grid, out_shape=shapes, in_specs=in_specs, ou...  12.8 us
    ppermute x4, starting transfers between devices, paired_sections(): return lax.ppermute(value, ('section', 'col'), pairs)  5.02 us
    ppermute x6, starting transfers between devices, swapped(): lax.ppermute(value, axis, [(source, source ^ distance) for source in rang...  4.28 us
    ppermute x6, waiting for transfers between devices, swapped(): lax.ppermute(value, axis, [(source, source ^ distance) for source in rang...  1.92 us
  transfers between devices with their start and end apart: 10, of which 3 were waited for; matrix products, arithmetic and copies ran while one was open for 0% of the time, Pallas kernels for 47%

profile of v8, /device:TPU:16, one launch (start us, length us, event | category | flops | bytes accessed | tf_op | source)
XLA Modules:
  0.0 25.3 jit_solution(2280969190993278263)
XLA Ops:
  0.6 0.0 copy-start
  0.6 1.6 %collective-permute-start.4 = (bf16[64,3072]{1,0:T(8,128)(2,1)}, bf16[64,3072]{1,0:T(8,128)(2,1)S(1)}, u32[]{:S(2)}, u32[]{:S(2)}) collective-permute-start(bf16[64,3072]{1,0:T(8,128)(2,1)} %bitcast.8), channel_id=1, source_target_pairs={{0,4},{4,0},{1,5},{5,1},{2,6},{6,2},{3,7},{7,3},{8,12},{12,8},{9,1... | collective-permute-start | bytes 1179656 | tf_op jit(solution)/shard_map/ppermute | solution.py:38
  2.2 1.5 %collective-permute-start.1 = (bf16[32,1536]{1,0:T(8,128)(2,1)}, bf16[32,1536]{1,0:T(8,128)(2,1)S(1)}, u32[]{:S(2)}, u32[]{:S(2)}) collective-permute-start(bf16[32,1536]{1,0:T(8,128)(2,1)} %bitcast.10), channel_id=1, source_target_pairs={{0,2},{1,3},{2,0},{3,1},{4,6},{5,7},{6,4},{7,5},{8,10},{9,11},{10,... | collective-permute-start | bytes 294920 | tf_op jit(solution)/shard_map/ppermute | solution.py:38
  3.7 3.9 %load.1 = (bf16[1536,3072]{1,0:T(8,128)(2,1)S(1)}, bf16[3072,1024]{1,0:T(8,128)(2,1)S(1)}, bf16[32,1536]{1,0:T(8,128)(2,1)S(1)}, bf16[64,3072]{1,0:T(8,128)(2,1)S(1)}) custom-call(bf16[1536,3072]{1,0:T(8,128)(2,1)} %bitcast.6, bf16[32,1536]{1,0:T(8,128)(2,1)} %bitcast.11, bf16[64,3072]{1,0:T(8,128)(2,1)} %bitcast.9), custom_call_target="tpu_custom_call" | custom-call | bytes 18874368 | tf_op jit(solution)/shard_map/load/pallas_call | solution.py:66
  7.7 0.0 collective-permute-done.1.across
  7.7 0.1 collective-permute-start.2
  7.8 0.0 copy-done
  7.8 0.5 %collective-permute-start = (bf16[32,1536]{1,0:T(8,128)(2,1)S(1)}, bf16[32,1536]{1,0:T(8,128)(2,1)S(1)}, u32[]{:S(2)}, u32[]{:S(2)}) collective-permute-start(bf16[32,1536]{1,0:T(8,128)(2,1)S(1)} %bitcast.12), channel_id=1, source_target_pairs={{0,1},{1,0},{2,3},{3,2},{4,5},{5,4},{6,7},{7,6},{8,9},{9,8},{10,11... | collective-permute-start | bytes 294920 | tf_op jit(solution)/shard_map/ppermute | solution.py:38
  8.3 1.0 %turn.1.second = bf16[3072,512]{1,0:T(8,128)(2,1)S(1)} custom-call(bf16[1536,3072]{1,0:T(8,128)(2,1)S(1)} %get-tuple-element.32.weight), custom_call_target="tpu_custom_call" | custom-call | flops 805306368 | bytes 6291456 | tf_op jit(solution)/shard_map/turn/pallas_call | solution.py:66
  9.3 0.0 collective-permute-done.2.diagonal
  9.3 0.0 collective-permute-done.beside
  9.3 1.4 %forward.1 = (bf16[128,1536]{1,0:T(8,128)(2,1)S(1)}, bf16[64,3072]{1,0:T(8,128)(2,1)S(1)}, bf16[64,3072]{1,0:T(8,128)(2,1)S(1)}) custom-call(bf16[32,1536]{1,0:T(8,128)(2,1)S(1)} %get-tuple-element.29.own, bf16[32,1536]{1,0:T(8,128)(2,1)S(1)} %collective-permute-done.beside, bf16[32,1536]{1,0:T(8,128)(2,1)S(1)} %collective-permute-done.1.across, ...), custom_call_target="tpu_custom_call" | custom-call | flops 1207959552 | bytes 9437184 | tf_op jit(solution)/shard_map/forward/pallas_call | solution.py:66
  10.7 0.6 %collective-permute-start.3 = (bf16[64,3072]{1,0:T(8,128)(2,1)S(1)}, bf16[64,3072]{1,0:T(8,128)(2,1)S(1)}, u32[]{:S(2)}, u32[]{:S(2)}) collective-permute-start(bf16[64,3072]{1,0:T(8,128)(2,1)S(1)} %get-tuple-element.35), channel_id=1, source_target_pairs={{0,4},{4,0},{1,5},{5,1},{2,6},{6,2},{3,7},{7,3},{8,12},{12,8},{9,1... | collective-permute-start | bytes 1179656 | tf_op jit(solution)/shard_map/ppermute | solution.py:38
  11.3 0.5 %collective-permute-done.4.other = bf16[64,3072]{1,0:T(8,128)(2,1)S(1)} collective-permute-done((bf16[64,3072]{1,0:T(8,128)(2,1)}, bf16[64,3072]{1,0:T(8,128)(2,1)S(1)}, u32[]{:S(2)}, u32[]{:S(2)}) %collective-permute-start.4) | collective-permute-done | bytes 393248 | tf_op jit(solution)/shard_map/ppermute | solution.py:38
  11.8 1.4 %input_grad.1 = (bf16[64,1536]{1,0:T(8,128)(2,1)S(1)}, f32[64,1536]{1,0:T(8,128)S(1)}) custom-call(bf16[64,3072]{1,0:T(8,128)(2,1)S(1)} %collective-permute-done.4.other, bf16[64,3072]{1,0:T(8,128)(2,1)S(1)} %get-tuple-element.37.own, bf16[3072,1024]{1,0:T(8,128)(2,1)S(1)} %get-tuple-element.38.first, bf16[3072,512]{1,0:T(8,128)(2,1)S(1)} %turn.1.second), custom_call_target="tpu_custom_call" | custom-call | flops 1207959552 | bytes 9437184 | tf_op jit(solution)/shard_map/input_grad/pallas_call | solution.py:66
  13.2 0.1 collective-permute-start.5
  13.2 1.4 %collective-permute-done.5.received = bf16[64,1536]{1,0:T(8,128)(2,1)S(1)} collective-permute-done((bf16[64,1536]{1,0:T(8,128)(2,1)S(1)}, bf16[64,1536]{1,0:T(8,128)(2,1)S(1)}, u32[]{:S(2)}, u32[]{:S(2)}) %collective-permute-start.5) | collective-permute-done | bytes 196640 | tf_op jit(solution)/shard_map/ppermute | solution.py:38
  14.7 1.6 %collective-permute-start.6 = (bf16[32,1536]{1,0:T(8,128)(2,1)S(1)}, bf16[32,1536]{1,0:T(8,128)(2,1)S(1)}, u32[]{:S(2)}, u32[]{:S(2)}) collective-permute-start(bf16[32,1536]{1,0:T(8,128)(2,1)S(1)} %get-tuple-element.48), channel_id=1, source_target_pairs={{0,8},{1,9},{2,10},{3,11},{8,0},{9,1},{10,2},{11,3},{16,24},{17,25... | collective-permute-start | bytes 294920 | tf_op jit(solution)/shard_map/ppermute | solution.py:33
  16.4 1.4 %collective-permute-start.7 = (bf16[32,1536]{1,0:T(8,128)(2,1)S(1)}, bf16[32,1536]{1,0:T(8,128)(2,1)S(1)}, u32[]{:S(2)}, u32[]{:S(2)}) collective-permute-start(bf16[32,1536]{1,0:T(8,128)(2,1)S(1)} %get-tuple-element.49), channel_id=1, source_target_pairs={{0,10},{1,11},{2,8},{3,9},{8,2},{9,3},{10,0},{11,1},{16,26},{17,27... | collective-permute-start | bytes 294920 | tf_op jit(solution)/shard_map/ppermute | solution.py:33
  17.7 0.4 %collective-permute-start.8 = (bf16[32,1536]{1,0:T(8,128)(2,1)S(1)}, bf16[32,1536]{1,0:T(8,128)(2,1)S(1)}, u32[]{:S(2)}, u32[]{:S(2)}) collective-permute-start(bf16[32,1536]{1,0:T(8,128)(2,1)S(1)} %get-tuple-element.50), channel_id=1, source_target_pairs={{0,1},{1,0},{2,3},{3,2},{8,18},{9,19},{10,16},{11,17},{16,10},{17,... | collective-permute-start | bytes 294920 | tf_op jit(solution)/shard_map/ppermute | solution.py:33
  18.2 1.6 %collective-permute-start.9 = (bf16[32,1536]{1,0:T(8,128)(2,1)S(1)}, bf16[32,1536]{1,0:T(8,128)(2,1)S(1)}, u32[]{:S(2)}, u32[]{:S(2)}) collective-permute-start(bf16[32,1536]{1,0:T(8,128)(2,1)S(1)} %get-tuple-element.51), channel_id=1, source_target_pairs={{0,1},{1,0},{2,3},{3,2},{8,16},{9,17},{10,18},{11,19},{16,8},{17,9... | collective-permute-start | bytes 294920 | tf_op jit(solution)/shard_map/ppermute | solution.py:33
  19.7 4.1 %weight_grad.1 = bf16[1536,3072]{1,0:T(8,128)(2,1)} custom-call(bf16[128,1536]{1,0:T(8,128)(2,1)S(1)} %get-tuple-element.46.tokens, bf16[64,3072]{1,0:T(8,128)(2,1)S(1)} %collective-permute-done.4.other, bf16[64,3072]{1,0:T(8,128)(2,1)S(1)} %get-tuple-element.37.own), custom_call_target="tpu_custom_call" | custom-call | flops 1207959552 | bytes 9437184 | tf_op jit(solution)/shard_map/weight_grad/pallas_call | solution.py:66
  23.9 0.0 collective-permute-done.3.received
  23.9 0.1 hidden_sum.1.hidden
  24.0 0.0 collective-permute-done.6.refs_0_
  24.0 0.0 collective-permute-done.7.refs_1_
  24.0 0.5 %collective-permute-done.8.refs_2_ = bf16[32,1536]{1,0:T(8,128)(2,1)S(1)} collective-permute-done((bf16[32,1536]{1,0:T(8,128)(2,1)S(1)}, bf16[32,1536]{1,0:T(8,128)(2,1)S(1)}, u32[]{:S(2)}, u32[]{:S(2)}) %collective-permute-start.8) | collective-permute-done | bytes 98336 | tf_op jit(solution)/shard_map/ppermute | solution.py:33
  24.5 0.0 collective-permute-done.9.refs_3_
  24.5 0.8 %final_sum.1 = (bf16[64,3072]{1,0:T(8,128)(2,1)}, bf16[32,1536]{1,0:T(8,128)(2,1)}) custom-call(bf16[64,3072]{1,0:T(8,128)(2,1)S(1)} %hidden_sum.1.hidden, bf16[32,1536]{1,0:T(8,128)(2,1)S(1)} %collective-permute-done.6.refs_0_, bf16[32,1536]{1,0:T(8,128)(2,1)S(1)} %collective-permute-done.7.refs_1_, bf16[32,1536]{1,0:T(8,128)(2,1)S(1)} %collective-permute-done.8.refs_2_, ...), custom_call_target="tpu_custom_call" | custom-call | bytes 1572864 | tf_op jit(solution)/shard_map/final_sum/pallas_call | solution.py:66
  (1 shorter events, 0.0 us)
Async XLA Ops:
  0.6 7.1 %copy-start = (bf16[1,32,1536]{2,1,0:T(8,128)(2,1)S(1)}, bf16[1,32,1536]{2,1,0:T(8,128)(2,1)}, u32[]{:S(2)}) copy-start(bf16[1,32,1536]{2,1,0:T(8,128)(2,1)} %param.3) | copy-start | bytes 294916
  0.6 11.1 %collective-permute-start.4 = (bf16[64,3072]{1,0:T(8,128)(2,1)}, bf16[64,3072]{1,0:T(8,128)(2,1)S(1)}, u32[]{:S(2)}, u32[]{:S(2)}) collective-permute-start(bf16[64,3072]{1,0:T(8,128)(2,1)} %bitcast.8), channel_id=1, source_target_pairs={{0,4},{4,0},{1,5},{5,1},{2,6},{6,2},{3,7},{7,3},{8,12},{12,8},{9,1... | collective-permute-start | bytes 1179656 | tf_op jit(solution)/shard_map/ppermute | solution.py:38
  2.2 5.4 %collective-permute-start.1 = (bf16[32,1536]{1,0:T(8,128)(2,1)}, bf16[32,1536]{1,0:T(8,128)(2,1)S(1)}, u32[]{:S(2)}, u32[]{:S(2)}) collective-permute-start(bf16[32,1536]{1,0:T(8,128)(2,1)} %bitcast.10), channel_id=1, source_target_pairs={{0,2},{1,3},{2,0},{3,1},{4,6},{5,7},{6,4},{7,5},{8,10},{9,11},{10,... | collective-permute-start | bytes 294920 | tf_op jit(solution)/shard_map/ppermute | solution.py:38
  7.7 1.6 %collective-permute-start.2 = (bf16[32,1536]{1,0:T(8,128)(2,1)S(1)}, bf16[32,1536]{1,0:T(8,128)(2,1)S(1)}, u32[]{:S(2)}, u32[]{:S(2)}) collective-permute-start(bf16[32,1536]{1,0:T(8,128)(2,1)S(1)} %collective-permute-done.1.across), channel_id=1, source_target_pairs={{0,1},{1,0},{2,3},{3,2},{4,5},{5,4},{6,7},{7,6},{8,9},{9,8},{10,11... | collective-permute-start | bytes 294920 | tf_op jit(solution)/shard_map/ppermute | solution.py:38
  7.8 1.5 %collective-permute-start = (bf16[32,1536]{1,0:T(8,128)(2,1)S(1)}, bf16[32,1536]{1,0:T(8,128)(2,1)S(1)}, u32[]{:S(2)}, u32[]{:S(2)}) collective-permute-start(bf16[32,1536]{1,0:T(8,128)(2,1)S(1)} %bitcast.12), channel_id=1, source_target_pairs={{0,1},{1,0},{2,3},{3,2},{4,5},{5,4},{6,7},{7,6},{8,9},{9,8},{10,11... | collective-permute-start | bytes 294920 | tf_op jit(solution)/shard_map/ppermute | solution.py:38
  10.7 13.2 %collective-permute-start.3 = (bf16[64,3072]{1,0:T(8,128)(2,1)S(1)}, bf16[64,3072]{1,0:T(8,128)(2,1)S(1)}, u32[]{:S(2)}, u32[]{:S(2)}) collective-permute-start(bf16[64,3072]{1,0:T(8,128)(2,1)S(1)} %get-tuple-element.35), channel_id=1, source_target_pairs={{0,4},{4,0},{1,5},{5,1},{2,6},{6,2},{3,7},{7,3},{8,12},{12,8},{9,1... | collective-permute-start | bytes 1179656 | tf_op jit(solution)/shard_map/ppermute | solution.py:38
  13.2 1.5 %collective-permute-start.5 = (bf16[64,1536]{1,0:T(8,128)(2,1)S(1)}, bf16[64,1536]{1,0:T(8,128)(2,1)S(1)}, u32[]{:S(2)}, u32[]{:S(2)}) collective-permute-start(bf16[64,1536]{1,0:T(8,128)(2,1)S(1)} %get-tuple-element.41), channel_id=1, source_target_pairs={{0,1},{1,0},{2,3},{3,2},{4,5},{5,4},{6,7},{7,6},{8,9},{9,8},{10,11... | collective-permute-start | bytes 589832 | tf_op jit(solution)/shard_map/ppermute | solution.py:38
  14.7 9.3 %collective-permute-start.6 = (bf16[32,1536]{1,0:T(8,128)(2,1)S(1)}, bf16[32,1536]{1,0:T(8,128)(2,1)S(1)}, u32[]{:S(2)}, u32[]{:S(2)}) collective-permute-start(bf16[32,1536]{1,0:T(8,128)(2,1)S(1)} %get-tuple-element.48), channel_id=1, source_target_pairs={{0,8},{1,9},{2,10},{3,11},{8,0},{9,1},{10,2},{11,3},{16,24},{17,25... | collective-permute-start | bytes 294920 | tf_op jit(solution)/shard_map/ppermute | solution.py:33
  16.4 7.6 %collective-permute-start.7 = (bf16[32,1536]{1,0:T(8,128)(2,1)S(1)}, bf16[32,1536]{1,0:T(8,128)(2,1)S(1)}, u32[]{:S(2)}, u32[]{:S(2)}) collective-permute-start(bf16[32,1536]{1,0:T(8,128)(2,1)S(1)} %get-tuple-element.49), channel_id=1, source_target_pairs={{0,10},{1,11},{2,8},{3,9},{8,2},{9,3},{10,0},{11,1},{16,26},{17,27... | collective-permute-start | bytes 294920 | tf_op jit(solution)/shard_map/ppermute | solution.py:33
  17.7 6.8 %collective-permute-start.8 = (bf16[32,1536]{1,0:T(8,128)(2,1)S(1)}, bf16[32,1536]{1,0:T(8,128)(2,1)S(1)}, u32[]{:S(2)}, u32[]{:S(2)}) collective-permute-start(bf16[32,1536]{1,0:T(8,128)(2,1)S(1)} %get-tuple-element.50), channel_id=1, source_target_pairs={{0,1},{1,0},{2,3},{3,2},{8,18},{9,19},{10,16},{11,17},{16,10},{17,... | collective-permute-start | bytes 294920 | tf_op jit(solution)/shard_map/ppermute | solution.py:33
  18.2 6.3 %collective-permute-start.9 = (bf16[32,1536]{1,0:T(8,128)(2,1)S(1)}, bf16[32,1536]{1,0:T(8,128)(2,1)S(1)}, u32[]{:S(2)}, u32[]{:S(2)}) collective-permute-start(bf16[32,1536]{1,0:T(8,128)(2,1)S(1)} %get-tuple-element.51), channel_id=1, source_target_pairs={{0,1},{1,0},{2,3},{3,2},{8,16},{9,17},{10,18},{11,19},{16,8},{17,9... | collective-permute-start | bytes 294920 | tf_op jit(solution)/shard_map/ppermute | solution.py:33
